TPU v7x, 512 devices: a whole 4x4x16 slice. The times are simulated.
512 devices in a mesh: map: 16 (over z), gx: 4 (over x_hi, core), gy: 8 (over x_lo, y).
Axes of the slice: x: 4 (x_hi: 2, x_lo: 2; x = x_hi * 2 + x_lo), y: 4, z: 16, core: 2. Of those that a mesh axis runs over, the one named last changes fastest.
Arguments:
- densities: float32 [16, 1536, 8192], P('map', 'gx', 'gy'), may hold values from 0.2 to 41, as said below
- scaling: float32 [16, 1536, 8192], P('map', 'gx', 'gy'), may hold values from 0.5 to 2
- weights: float32 [16], P('map'), as said below
Outputs:
- barycenter: float32 [1536, 8192], P('gx', 'gy')
- new_scaling: float32 [16, 1536, 8192], P('map', 'gx', 'gy')
Inputs may be any that keep to these rules, and one draw needn't show every extreme that they name: `densities`: every cell's demand density is positive. The weights are positive and sum to one.
All inputs are finite; a program needn't handle non-finite values.
Results may differ from a plain program's by a relative error of at most 0.0001.
Values sent between devices are 32-bit elements; how exact they have to be, the bound alone decides.
A program may use at most 64 MiB of HBM per device.

v0:
```python
import jax
import jax.numpy as jnp
from jax import lax
from jax.sharding import PartitionSpec as P

HALF = 32
SIGMA = 16


def extended(block, sides, width):
    for axis, dim in sides:
        count = lax.axis_size(axis)
        forward = [(i, i + 1) for i in range(count - 1)]
        backward = [(target, source) for source, target in forward]
        low = lax.ppermute(
            lax.slice_in_dim(block, block.shape[dim] - width, None, axis=dim), axis, forward
        )
        high = lax.ppermute(lax.slice_in_dim(block, 0, width, axis=dim), axis, backward)
        block = jnp.concatenate([low, block, high], axis=dim)
    return block


def kernel_band(count):
    rows = jnp.arange(count, dtype=jnp.int32)[:, None]
    cols = jnp.arange(count + 2 * HALF, dtype=jnp.int32)[None, :]
    offset = (cols - rows - HALF).astype(jnp.float32)
    inside = jnp.abs(cols - rows - HALF) <= HALF
    taps = jnp.arange(2 * HALF + 1, dtype=jnp.float32) - HALF
    total = jnp.sum(jnp.exp(-taps * taps / (2.0 * SIGMA * SIGMA)))
    values = jnp.exp(-offset * offset / (2.0 * SIGMA * SIGMA)) / total
    return jnp.where(inside, values, jnp.float32(0.0))


def smooth_axis(padded, axis, length):
    block = min(128, length)
    nblocks = length // block
    pieces = -(-(block + 2 * HALF) // block)
    extra = (nblocks + pieces - 1) * block - (length + 2 * HALF)
    widths = [(0, 0)] * padded.ndim
    widths[axis] = (0, extra)
    padded = jnp.pad(padded, widths)
    band = kernel_band(block)
    band = jnp.pad(band, ((0, 0), (0, pieces * block - block - 2 * HALF)))
    result = None
    for index in range(pieces):
        piece = lax.slice_in_dim(padded, index * block, index * block + length, axis=axis)
        small = band[:, index * block : (index + 1) * block]
        if axis == 1:
            piece = piece.reshape(piece.shape[0], nblocks, block, piece.shape[2])
            term = jnp.einsum(
                "ic,mbcj->mbij",
                small,
                piece,
                precision=lax.Precision.HIGHEST,
                preferred_element_type=jnp.float32,
            )
        else:
            piece = piece.reshape(piece.shape[0], piece.shape[1], nblocks, block)
            term = jnp.einsum(
                "mibc,kc->mibk",
                piece,
                small,
                precision=lax.Precision.HIGHEST,
                preferred_element_type=jnp.float32,
            )
        result = term if result is None else result + term
    if axis == 1:
        return result.reshape(result.shape[0], length, result.shape[3])
    return result.reshape(result.shape[0], result.shape[1], length)


def convolve(field):
    tile_rows = field.shape[1]
    tile_cols = field.shape[2]
    padded = extended(field, (("gx", 1), ("gy", 2)), HALF)
    rows_done = smooth_axis(padded, 1, tile_rows)
    return smooth_axis(rows_done, 2, tile_cols)


def local(densities, scaling, weights):
    tile_rows = densities.shape[1]
    tile_cols = densities.shape[2]
    kv = convolve(scaling)
    u_field = densities / kv
    ku = convolve(u_field)
    partial_log = jnp.sum(weights[:, None, None] * jnp.log(scaling * ku), axis=0)
    cells = jnp.float32(tile_rows * tile_cols * lax.axis_size("gx") * lax.axis_size("gy"))
    logsum = lax.psum(partial_log, "map")
    raw = jnp.exp(logsum)
    mass = lax.psum(jnp.sum(raw), ("gx", "gy"))
    barycenter = cells * raw / mass
    new_scaling = barycenter[None, :, :] / ku
    return (barycenter, new_scaling)


def solution(mesh):
    placed = (P("map", "gx", "gy"), P("map", "gx", "gy"), P("map"))
    return jax.shard_map(
        local,
        mesh=mesh,
        in_specs=placed,
        out_specs=(P("gx", "gy"), P("map", "gx", "gy")),
        check_vma=False,
    )
```

profile of v0, /device:TPU:6, one launch (start us, length us, event | category | flops | bytes accessed | tf_op | source)
XLA Modules:
  0.0 329.5 jit_solution(6116755985501494899)
XLA Ops:
  8.2 1.9 collective-permute-start
  10.1 5.1 %collective-permute-start.1 = (f32[1,32,1024]{2,1,0:T(8,128)S(1)}, f32[1,32,1024]{2,1,0:T(8,128)S(1)}, u32[]{:S(2)}, u32[]{:S(2)}) collective-permute-start(f32[1,32,1024]{2,1,0:T(8,128)S(1)} %get-tuple-element.18), channel_id=1, source_target_pairs={{8,0},{16,8},{24,16},{9,1},{17,9},{25,17},{10,2},{18,10},{26,18},{... | collective-permute-start | bytes 393224 | tf_op jit(solution)/shard_map/ppermute | solution.py:18
  17.9 3.5 %collective-permute-start.2 = (f32[1,448,32]{2,1,0:T(8,128)S(1)}, f32[1,448,32]{2,1,0:T(8,128)S(1)}, u32[]{:S(2)}, u32[]{:S(2)}) collective-permute-start(f32[1,448,32]{2,1,0:T(8,128)S(1)} %get-tuple-element.9), channel_id=1, source_target_pairs={{0,1},{1,2},{2,3},{3,4},{4,5},{5,6},{6,7},{8,9},{9,10},{10,11},{11... | collective-permute-start | bytes 172040 | tf_op jit(solution)/shard_map/ppermute | solution.py:15
  21.4 4.5 %collective-permute-start.3 = (f32[1,448,32]{2,1,0:T(8,128)S(1)}, f32[1,448,32]{2,1,0:T(8,128)S(1)}, u32[]{:S(2)}, u32[]{:S(2)}) collective-permute-start(f32[1,448,32]{2,1,0:T(8,128)S(1)} %get-tuple-element.8), channel_id=1, source_target_pairs={{1,0},{2,1},{3,2},{4,3},{5,4},{6,5},{7,6},{9,8},{10,9},{11,10},{12... | collective-permute-start | bytes 172040 | tf_op jit(solution)/shard_map/ppermute | solution.py:18
  29.4 2.9 concatenate.13
  32.6 3.0 fusion.13
  35.6 3.8 %fusion = f32[1,3,128,1088]{2,3,1,0:T(8,128)S(1)} fusion(f32[3,1088,128]{2,1,0:T(8,128)S(1)} %fusion.13, f32[3,128,1088]{2,1,0:T(8,128)S(1)} %bitcast.50, f32[128,192]{1,0:T(8,128)} %copy-done.2), kind=kOutput, calls=%fused_computation.2 | convolution fusion | flops 642146304 | bytes 5079040 | tf_op jit(solution)/shard_map/ic,mbcj->mbij/dot_general | solution.py:50
  42.0 1.9 copy.11
  43.9 2.7 fusion.8
  46.6 1.6 copy.13
  48.2 2.9 convolution_add_fusion.3
  51.6 1.7 div.45
  53.3 1.9 collective-permute-start.4
  55.3 5.1 %collective-permute-start.5 = (f32[1,32,1024]{2,1,0:T(8,128)S(1)}, f32[1,32,1024]{2,1,0:T(8,128)S(1)}, u32[]{:S(2)}, u32[]{:S(2)}) collective-permute-start(f32[1,32,1024]{2,1,0:T(8,128)S(1)} %get-tuple-element.17), channel_id=1, source_target_pairs={{8,0},{16,8},{24,16},{9,1},{17,9},{25,17},{10,2},{18,10},{26,18},{... | collective-permute-start | bytes 393224 | tf_op jit(solution)/shard_map/ppermute | solution.py:18
  61.1 1.8 collective-permute-done.5
  63.3 3.4 %collective-permute-start.6 = (f32[1,448,32]{2,1,0:T(8,128)S(1)}, f32[1,448,32]{2,1,0:T(8,128)S(1)}, u32[]{:S(2)}, u32[]{:S(2)}) collective-permute-start(f32[1,448,32]{2,1,0:T(8,128)S(1)} %get-tuple-element.7), channel_id=1, source_target_pairs={{0,1},{1,2},{2,3},{3,4},{4,5},{5,6},{6,7},{8,9},{9,10},{10,11},{11... | collective-permute-start | bytes 172040 | tf_op jit(solution)/shard_map/ppermute | solution.py:15
  66.7 6.6 %collective-permute-start.7 = (f32[1,448,32]{2,1,0:T(8,128)S(1)}, f32[1,448,32]{2,1,0:T(8,128)S(1)}, u32[]{:S(2)}, u32[]{:S(2)}) collective-permute-start(f32[1,448,32]{2,1,0:T(8,128)S(1)} %get-tuple-element.6), channel_id=1, source_target_pairs={{1,0},{2,1},{3,2},{4,3},{5,4},{6,5},{7,6},{9,8},{10,9},{11,10},{12... | collective-permute-start | bytes 172040 | tf_op jit(solution)/shard_map/ppermute | solution.py:18
  76.6 2.9 concatenate.15
  79.8 3.0 fusion.10
  82.8 3.0 fusion.1
  88.3 1.9 copy.19
  90.3 2.7 fusion.7
  92.9 1.6 copy.21
  94.5 3.4 %convolution_add_fusion.2 = f32[384,8,128]{0,2,1:T(8,128)S(1)} fusion(f32[384,8,128]{0,2,1:T(8,128)} %fusion.7, f32[384,8,128]{0,2,1:T(8,128)} %bitcast.56, f32[128,192]{1,0:T(8,128)S(1)} %copy-done.5), kind=kOutput, calls=%fused_computation.11 | convolution fusion | flops 604372992 | bytes 4816896 | tf_op jit(solution)/shard_map/mibc,kc->mibk/dot_general | solution.py:59
  97.9 1.6 copy.23
  99.6 2.9 multiply_bitcast_fusion
  102.5 147.3 %all-reduce.7.cloned.1.call-done = f32[384,1024]{1,0:T(8,128)} async-done(((f32[384,1024]{1,0:T(8,128)}), f32[384,1024]{1,0:T(8,128)}) %all-reduce.7.cloned.1.call-update) | async-done | bytes 1572880 | tf_op jit(solution)/shard_map/psum | solution.py:88
  249.8 2.4 exponential_reduce_fusion
  252.2 63.7 %psum.15 = f32[]{:T(128)} all-reduce(f32[]{:T(128)} %exponential_reduce_fusion), channel_id=1, replica_groups=mesh['map'=16,'gx'=4,'gy'=8] {'gx','gy'}, use_global_device_ids=true, to_apply=%region_3.4 | all-reduce | flops 1 | bytes 8 | tf_op jit(solution)/shard_map/psum | solution.py:90
  316.0 2.0 broadcast_multiply_fusion
  317.9 2.0 copy.24
  319.9 2.8 divide_bitcast_fusion
  (44 shorter events, 17.0 us)
Async XLA Ops:
  7.2 242.6 %all-reduce.7.cloned.1.call-start = ((), (), s32[]{:S(2)}) async-start(), calls=%async_computation | async-start | bytes 3145728 | tf_op jit(solution)/shard_map/psum | solution.py:88
  8.2 7.8 %collective-permute-start = (f32[1,32,1024]{2,1,0:T(8,128)S(1)}, f32[1,32,1024]{2,1,0:T(8,128)S(1)}, u32[]{:S(2)}, u32[]{:S(2)}) collective-permute-start(f32[1,32,1024]{2,1,0:T(8,128)S(1)} %get-tuple-element.19), channel_id=1, source_target_pairs={{0,8},{8,16},{16,24},{1,9},{9,17},{17,25},{2,10},{10,18},{18,26},{... | collective-permute-start | bytes 393224 | tf_op jit(solution)/shard_map/ppermute | solution.py:15
  10.1 7.7 %collective-permute-start.1 = (f32[1,32,1024]{2,1,0:T(8,128)S(1)}, f32[1,32,1024]{2,1,0:T(8,128)S(1)}, u32[]{:S(2)}, u32[]{:S(2)}) collective-permute-start(f32[1,32,1024]{2,1,0:T(8,128)S(1)} %get-tuple-element.18), channel_id=1, source_target_pairs={{8,0},{16,8},{24,16},{9,1},{17,9},{25,17},{10,2},{18,10},{26,18},{... | collective-permute-start | bytes 393224 | tf_op jit(solution)/shard_map/ppermute | solution.py:18
  17.8 10.2 %copy-start.8 = (f32[1,448,1024]{2,1,0:T(8,128)}, f32[1,448,1024]{2,1,0:T(8,128)S(1)}, u32[]{:S(2)}) copy-start(f32[1,448,1024]{2,1,0:T(8,128)S(1)} %constant_dynamic-update-slice_fusion) | copy-start | bytes 5505028
  17.9 10.0 %collective-permute-start.2 = (f32[1,448,32]{2,1,0:T(8,128)S(1)}, f32[1,448,32]{2,1,0:T(8,128)S(1)}, u32[]{:S(2)}, u32[]{:S(2)}) collective-permute-start(f32[1,448,32]{2,1,0:T(8,128)S(1)} %get-tuple-element.9), channel_id=1, source_target_pairs={{0,1},{1,2},{2,3},{3,4},{4,5},{5,6},{6,7},{8,9},{9,10},{10,11},{11... | collective-permute-start | bytes 172040 | tf_op jit(solution)/shard_map/ppermute | solution.py:15
  21.4 8.0 %collective-permute-start.3 = (f32[1,448,32]{2,1,0:T(8,128)S(1)}, f32[1,448,32]{2,1,0:T(8,128)S(1)}, u32[]{:S(2)}, u32[]{:S(2)}) collective-permute-start(f32[1,448,32]{2,1,0:T(8,128)S(1)} %get-tuple-element.8), channel_id=1, source_target_pairs={{1,0},{2,1},{3,2},{4,3},{5,4},{6,5},{7,6},{9,8},{10,9},{11,10},{12... | collective-permute-start | bytes 172040 | tf_op jit(solution)/shard_map/ppermute | solution.py:18
  26.6 6.0 %copy-start.2 = (f32[128,192]{1,0:T(8,128)}, f32[128,192]{1,0:T(8,128)S(1)}, u32[]{:S(2)}) copy-start(f32[128,192]{1,0:T(8,128)S(1)} %fusion.5) | copy-start | bytes 294916
  42.0 1.9 copy-start.3
  46.6 1.6 copy-start.7
  53.3 7.8 %collective-permute-start.4 = (f32[1,32,1024]{2,1,0:T(8,128)S(1)}, f32[1,32,1024]{2,1,0:T(8,128)S(1)}, u32[]{:S(2)}, u32[]{:S(2)}) collective-permute-start(f32[1,32,1024]{2,1,0:T(8,128)S(1)} %get-tuple-element.16), channel_id=1, source_target_pairs={{0,8},{8,16},{16,24},{1,9},{9,17},{17,25},{2,10},{10,18},{18,26},{... | collective-permute-start | bytes 393224 | tf_op jit(solution)/shard_map/ppermute | solution.py:15
  55.3 7.7 %collective-permute-start.5 = (f32[1,32,1024]{2,1,0:T(8,128)S(1)}, f32[1,32,1024]{2,1,0:T(8,128)S(1)}, u32[]{:S(2)}, u32[]{:S(2)}) collective-permute-start(f32[1,32,1024]{2,1,0:T(8,128)S(1)} %get-tuple-element.17), channel_id=1, source_target_pairs={{8,0},{16,8},{24,16},{9,1},{17,9},{25,17},{10,2},{18,10},{26,18},{... | collective-permute-start | bytes 393224 | tf_op jit(solution)/shard_map/ppermute | solution.py:18
  63.1 12.0 %copy-start = (f32[1,448,1024]{2,1,0:T(8,128)}, f32[1,448,1024]{2,1,0:T(8,128)S(1)}, u32[]{:S(2)}) copy-start(f32[1,448,1024]{2,1,0:T(8,128)S(1)} %pad_maximum_fusion) | copy-start | bytes 5505028
  63.3 11.9 %collective-permute-start.6 = (f32[1,448,32]{2,1,0:T(8,128)S(1)}, f32[1,448,32]{2,1,0:T(8,128)S(1)}, u32[]{:S(2)}, u32[]{:S(2)}) collective-permute-start(f32[1,448,32]{2,1,0:T(8,128)S(1)} %get-tuple-element.7), channel_id=1, source_target_pairs={{0,1},{1,2},{2,3},{3,4},{4,5},{5,6},{6,7},{8,9},{9,10},{10,11},{11... | collective-permute-start | bytes 172040 | tf_op jit(solution)/shard_map/ppermute | solution.py:15
  66.7 9.9 %collective-permute-start.7 = (f32[1,448,32]{2,1,0:T(8,128)S(1)}, f32[1,448,32]{2,1,0:T(8,128)S(1)}, u32[]{:S(2)}, u32[]{:S(2)}) collective-permute-start(f32[1,448,32]{2,1,0:T(8,128)S(1)} %get-tuple-element.6), channel_id=1, source_target_pairs={{1,0},{2,1},{3,2},{4,3},{5,4},{6,5},{7,6},{9,8},{10,9},{11,10},{12... | collective-permute-start | bytes 172040 | tf_op jit(solution)/shard_map/ppermute | solution.py:18
  79.8 3.0 copy-start.4
  88.3 1.9 copy-start.5
  97.9 1.6 copy-start.1
  317.9 2.0 copy-start.6
Sparse Core Ops, SparseCore 0:
  102.6 147.1 all-reduce.6
where the time goes:
time: 331 us; the launch traced here: 330 us
  waiting for transfers between devices  156 us (47%)
  blocking collectives  63.7 us (19%)
  starting transfers between devices  32.1 us (10%)
  local copies, waits for them, and re-layouts  25.4 us (8%)
  matrix products  24.4 us (7%)
  between operations  15 us (5%)
  other arithmetic  13.2 us (4%)
    psum x1, waiting for transfers between devices, local(): logsum = lax.psum(partial_log, 'map')  147 us
    psum x1, blocking collectives, local(): mass = lax.psum(jnp.sum(raw), ('gx', 'gy'))  63.7 us
    ppermute x4, starting transfers between devices, extended(): lax.ppermute(lax.slice_in_dim(block, 0, width, axis=dim), axis, backward)  21.3 us
    dot_general x4, matrix products, smooth_axis(): jnp.einsum('ic,mbcj->mbij', small, piece, precision=lax.Precision.HIGHEST...  12.8 us
    dot_general x4, matrix products, smooth_axis(): jnp.einsum('mibc,kc->mibk', piece, small, precision=lax.Precision.HIGHEST...  11.6 us
    ppermute x4, starting transfers between devices, extended(): lax.ppermute(lax.slice_in_dim(block, block.shape[dim] - width, None, axis...  10.7 us
    slice x8, local copies, waits for them, and re-layouts, smooth_axis(): lax.slice_in_dim(padded, index * block, index * block + length, axis=axis)  10.3 us
  transfers between devices with their start and end apart: 9, of which 9 were waited for; matrix products, arithmetic and copies ran while one was open for 1% of the time, Pallas kernels for 0%

commit v1 on v0

v1 whole, which is shorter than its diff:
```python
import functools

import jax
import jax.numpy as jnp
import ml_dtypes
import numpy as np
from jax import lax
from jax.experimental import pallas as pl
from jax.experimental.pallas import tpu as pltpu
from jax.sharding import PartitionSpec as P

HALF = 32
SIGMA = 16
LANES = 128
BLOCK = 256
SUBS = 2
MESH = pl.DeviceIdType.MESH


def band(count_out, count_in, shift):
    taps = np.arange(-HALF, HALF + 1, dtype=np.float64)
    total = np.sum(np.exp(-taps * taps / (2.0 * SIGMA * SIGMA)))
    offset = np.arange(count_in)[None, :] - np.arange(count_out)[:, None] - shift
    values = np.exp(-(offset.astype(np.float64) ** 2) / (2.0 * SIGMA * SIGMA)) / total
    values = np.where(np.abs(offset) <= HALF, values, 0.0)
    high = values.astype(ml_dtypes.bfloat16)
    low = (values - high.astype(np.float64)).astype(ml_dtypes.bfloat16)
    return np.stack([high, low])


def split(x):
    high = x.astype(jnp.bfloat16)
    low = (x - high.astype(jnp.float32)).astype(jnp.bfloat16)
    return high, low


def dot(a, b):
    return jnp.dot(a, b, preferred_element_type=jnp.float32)


def dot3(a_high, a_low, b_high, b_low):
    return dot(a_high, b_high) + (dot(a_high, b_low) + dot(a_low, b_high))


def kernel(
    sizes,
    rows,
    cols,
    s_hbm,
    d_hbm,
    w_ref,
    brow1,
    brow2,
    bcol,
    raw_ref,
    ku_ref,
    norm_ref,
    s_ext,
    d_ext,
    y_high,
    y_low,
    u_high,
    u_low,
    term,
    pack,
    strip,
    cw,
    ccw,
    m_out,
    m_gx,
    m_gy,
    m_map,
    in_sem,
    halo_send,
    halo_recv,
    cw_send,
    cw_recv,
    ccw_send,
    ccw_recv,
    acw_send,
    acw_recv,
    accw_send,
    accw_recv,
    m_gx_sem,
    m_gy_sem,
    m_map_sem,
):
    n, ngx, ngy = sizes
    z, gx, gy = lax.axis_index("map"), lax.axis_index("gx"), lax.axis_index("gy")
    wide = 2 * HALF
    left, right = LANES, LANES + cols
    s_top, s_bottom = wide, wide + rows
    d_top, d_bottom = HALF, HALF + rows

    load_s = pltpu.make_async_copy(
        s_hbm.at[0], s_ext.at[pl.ds(s_top, rows), pl.ds(left, cols)], in_sem.at[0]
    )
    load_d = pltpu.make_async_copy(
        d_hbm.at[0], d_ext.at[pl.ds(d_top, rows), pl.ds(left, cols)], in_sem.at[1]
    )
    load_s.start()
    load_d.start()

    near = []
    for dx in (-1, 0, 1):
        for dy in (-1, 0, 1):
            if dx or dy:
                ok = (gx + dx >= 0) & (gx + dx < ngx) & (gy + dy >= 0) & (gy + dy < ngy)
                near.append((dx, dy, ok))

    barrier = pltpu.get_barrier_semaphore()
    expected = jnp.int32(0)
    for dx, dy, ok in near:
        expected = expected + ok.astype(jnp.int32)

        @pl.when(ok)
        def _():
            pl.semaphore_signal(
                barrier, inc=1, device_id={"gx": gx + dx, "gy": gy + dy}, device_id_type=MESH
            )

    for axis, me, count in (("gx", gx, ngx), ("gy", gy, ngy), ("map", z, n)):
        for k in range(1, count):
            pl.semaphore_signal(
                barrier,
                inc=1,
                device_id={axis: lax.rem(me + k, count)},
                device_id_type=MESH,
            )
        expected = expected + (count - 1)
    pl.semaphore_wait(barrier, expected)

    def side(delta):
        return 0 if delta > 0 else 1

    def row_copies(dx):
        first = 0 if dx < 0 else rows - wide
        s_at = s_bottom if dx < 0 else 0
        d_first = 0 if dx < 0 else rows - HALF
        d_at = d_bottom if dx < 0 else 0
        slot = side(dx)
        to = {"gx": gx + dx}
        return (
            pltpu.make_async_remote_copy(
                s_hbm.at[0, pl.ds(first, wide)],
                s_ext.at[pl.ds(s_at, wide), pl.ds(left, cols)],
                halo_send.at[slot],
                halo_recv.at[slot],
                device_id=to,
                device_id_type=MESH,
            ),
            pltpu.make_async_remote_copy(
                d_hbm.at[0, pl.ds(d_first, HALF)],
                d_ext.at[pl.ds(d_at, HALF), pl.ds(left, cols)],
                halo_send.at[2 + slot],
                halo_recv.at[2 + slot],
                device_id=to,
                device_id_type=MESH,
            ),
        )

    def col_copy(dx, dy):
        if dx == 0:
            src, at, size, slot = 0, s_top, rows, 4 + side(dy)
        else:
            src = 0 if dx < 0 else rows - wide
            at, size = (s_bottom if dx < 0 else 0), wide
            slot = 6 + 2 * side(dx) + side(dy)
        return pltpu.make_async_remote_copy(
            pack.at[side(dy), pl.ds(src, size)],
            strip.at[side(dy), pl.ds(at, size)],
            halo_send.at[slot],
            halo_recv.at[slot],
            device_id={"gx": gx + dx, "gy": gy + dy},
            device_id_type=MESH,
        )

    for dx, dy, ok in near:
        if dy == 0:

            @pl.when(ok)
            def _():
                for copy in row_copies(dx):
                    copy.start()

    load_s.wait()
    load_d.wait()
    lane = lax.broadcasted_iota(jnp.int32, (rows, LANES), 1)
    s_last = s_ext[pl.ds(s_top, rows), pl.ds(right - LANES, LANES)]
    d_last = d_ext[pl.ds(d_top, rows), pl.ds(right - LANES, LANES)]
    pack[0] = jnp.where(lane >= wide, s_last, pltpu.roll(d_last, wide, 1))
    s_first = s_ext[pl.ds(s_top, rows), pl.ds(left, LANES)]
    d_first = d_ext[pl.ds(d_top, rows), pl.ds(left, LANES)]
    pack[1] = jnp.where(lane < wide, s_first, pltpu.roll(d_first, wide, 1))

    for dx, dy, ok in near:
        if dy != 0:

            @pl.when(ok)
            def _():
                col_copy(dx, dy).start()

    for dx, dy, ok in near:
        if dy == 0:

            @pl.when(jnp.logical_not(ok))
            def _():
                at = 0 if dx < 0 else s_bottom
                s_ext[pl.ds(at, wide), pl.ds(left, cols)] = jnp.zeros((wide, cols), jnp.float32)

        else:

            @pl.when(jnp.logical_not(ok))
            def _():
                at = s_top if dx == 0 else (0 if dx < 0 else s_bottom)
                size = rows if dx == 0 else wide
                strip[0 if dy < 0 else 1, pl.ds(at, size)] = jnp.zeros(
                    (size, LANES), jnp.float32
                )

    for dx, dy, ok in near:
        @pl.when(ok)
        def _():
            if dy == 0:
                for copy in row_copies(-dx):
                    copy.wait_recv()
            else:
                col_copy(-dx, -dy).wait_recv()

    s_ext[:, pl.ds(0, LANES)] = strip[0]
    s_ext[:, pl.ds(right, LANES)] = strip[1]
    mid = rows + wide
    d_ext[:, pl.ds(0, LANES)] = pltpu.roll(strip[0, pl.ds(HALF, mid)], wide, 1)
    d_ext[:, pl.ds(right, LANES)] = pltpu.roll(strip[1, pl.ds(HALF, mid)], wide, 1)

    frame = cols + 2 * LANES

    def row_pass1(block, carry):
        at = pl.ds(pl.multiple_of(block * BLOCK, BLOCK), BLOCK)
        high, low = split(s_ext[:, at])
        out = dot3(brow1[0], brow1[1], high, low)
        y_high[:, at], y_low[:, at] = split(out)
        return carry

    lax.fori_loop(0, frame // BLOCK, row_pass1, 0)

    def col_pass(count, base, first, size_in, size_out):
        source = pl.ds(base, size_in)
        b_high = bcol[0, pl.ds(first, size_in), pl.ds(0, size_out)]
        b_low = bcol[1, pl.ds(first, size_in), pl.ds(0, size_out)]
        return dot3(y_high[pl.ds(0, count), source], y_low[pl.ds(0, count), source], b_high, b_low)

    def u_block(block, carry):
        base = pl.multiple_of(block * BLOCK, BLOCK)
        at = pl.ds(pl.multiple_of(base + LANES, LANES), BLOCK)
        kv = col_pass(mid, base, 0, 2 * BLOCK, BLOCK)
        u_high[:, at], u_low[:, at] = split(d_ext[:, at] / kv)
        return carry

    lax.fori_loop(0, cols // BLOCK, u_block, 0)

    lane = lax.broadcasted_iota(jnp.int32, (mid, LANES), 1)
    for at, base, first, keep in (
        (0, 0, LANES, (lane >= LANES - HALF) & (gy > 0)),
        (right, right - LANES, 0, (lane < HALF) & (gy < ngy - 1)),
    ):
        kv = col_pass(mid, base, first, BLOCK, LANES)
        value = jnp.where(keep, d_ext[:, pl.ds(at, LANES)] / kv, jnp.float32(0.0))
        u_high[:, pl.ds(at, LANES)], u_low[:, pl.ds(at, LANES)] = split(value)

    for edge, at in ((gx == 0, 0), (gx == ngx - 1, d_bottom)):

        @pl.when(edge)
        def _():
            zero = jnp.zeros((HALF, frame), jnp.bfloat16)
            u_high[pl.ds(at, HALF), :] = zero
            u_low[pl.ds(at, HALF), :] = zero

    def row_pass2(block, carry):
        at = pl.ds(pl.multiple_of(block * BLOCK, BLOCK), BLOCK)
        out = dot3(brow2[0], brow2[1], u_high[:, at], u_low[:, at])
        y_high[pl.ds(0, rows), at], y_low[pl.ds(0, rows), at] = split(out)
        return carry

    lax.fori_loop(0, frame // BLOCK, row_pass2, 0)

    weight = w_ref[0]

    def ku_block(block, carry):
        base = pl.multiple_of(block * BLOCK, BLOCK)
        ku = col_pass(rows, base, 0, 2 * BLOCK, BLOCK)
        ku_ref[:, pl.ds(base, BLOCK)] = ku
        inner = s_ext[
            pl.ds(s_top, rows), pl.ds(pl.multiple_of(base + LANES, LANES), BLOCK)
        ]
        term[:, pl.ds(base, BLOCK)] = weight * jnp.log(inner * ku)
        return carry

    lax.fori_loop(0, cols // BLOCK, ku_block, 0)

    size = rows // n
    width = cols // SUBS
    far, close = n // 2, (n - 1) // 2
    after, before = lax.rem(z + 1, n), lax.rem(z + n - 1, n)

    def chunk(d):
        return pl.ds(pl.multiple_of(lax.rem(d + 2 * n, n) * size, 8), size)

    def lanes(sub):
        return pl.ds(sub * width, width)

    def cw_copy(src, step, sub):
        return pltpu.make_async_remote_copy(
            src,
            cw.at[step, :, lanes(sub)],
            cw_send.at[step, sub],
            cw_recv.at[step, sub],
            device_id={"map": after},
            device_id_type=MESH,
        )

    def ccw_copy(src, step, sub):
        return pltpu.make_async_remote_copy(
            src,
            ccw.at[step, :, lanes(sub)],
            ccw_send.at[step, sub],
            ccw_recv.at[step, sub],
            device_id={"map": before},
            device_id_type=MESH,
        )

    def cw_next(step, sub):
        cw_copy(cw.at[step - 1, :, lanes(sub)], step - 1, sub).wait_recv()
        cw[step - 1, :, lanes(sub)] += term[chunk(z + far - step), lanes(sub)]
        cw_copy(cw.at[step - 1, :, lanes(sub)], step, sub).start()

    def ccw_next(step, sub):
        ccw_copy(ccw.at[step - 1, :, lanes(sub)], step - 1, sub).wait_recv()
        ccw[step - 1, :, lanes(sub)] += term[chunk(z - close + step), lanes(sub)]
        ccw_copy(ccw.at[step - 1, :, lanes(sub)], step, sub).start()

    for sub in range(SUBS):
        cw_copy(term.at[chunk(z + far), lanes(sub)], 0, sub).start()
        if close > 0:
            ccw_copy(term.at[chunk(z - close), lanes(sub)], 0, sub).start()

    def ring(step, carry):
        for sub in range(SUBS):
            cw_next(step, sub)
            ccw_next(step, sub)
        return carry

    lax.fori_loop(1, close, ring, 0)
    for step in range(max(close, 1), far):
        for sub in range(SUBS):
            cw_next(step, sub)

    def acw_copy(step, sub):
        ref = raw_ref.at[chunk(z - step), lanes(sub)]
        return pltpu.make_async_remote_copy(
            ref,
            ref,
            acw_send.at[step, sub],
            acw_recv.at[step, sub],
            device_id={"map": after},
            device_id_type=MESH,
        )

    def accw_copy(step, sub):
        ref = raw_ref.at[chunk(z + step), lanes(sub)]
        return pltpu.make_async_remote_copy(
            ref,
            ref,
            accw_send.at[step, sub],
            accw_recv.at[step, sub],
            device_id={"map": before},
            device_id_type=MESH,
        )

    partial = jnp.zeros((8, LANES), jnp.float32)
    for sub in range(SUBS):
        cw_copy(cw.at[far - 1, :, lanes(sub)], far - 1, sub).wait_recv()
        value = term[chunk(z), lanes(sub)] + cw[far - 1, :, lanes(sub)]
        if close > 0:
            ccw_copy(ccw.at[close - 1, :, lanes(sub)], close - 1, sub).wait_recv()
            value = value + ccw[close - 1, :, lanes(sub)]
        value = jnp.exp(value)
        raw_ref[chunk(z), lanes(sub)] = value
        acw_copy(0, sub).start()
        if close > 0:
            accw_copy(0, sub).start()
        for i in range(size // 8):
            for j in range(width // LANES):
                partial = partial + value[
                    i * 8 : (i + 1) * 8, j * LANES : (j + 1) * LANES
                ]

    def mass_copies(stage, axis, me, count, slots, sems):
        return [
            pltpu.make_async_remote_copy(
                m_out.at[stage],
                slots.at[me],
                sems.at[0, k],
                sems.at[1, me],
                device_id={axis: lax.rem(me + k, count)},
                device_id_type=MESH,
            )
            for k in range(1, count)
        ]

    def mass_start(stage, axis, me, count, slots, sems, value):
        m_out[stage] = value
        slots[me] = value
        for copy in mass_copies(stage, axis, me, count, slots, sems):
            copy.start()

    def mass_finish(stage, axis, me, count, slots, sems):
        for k in range(1, count):
            source = lax.rem(me + k, count)
            pltpu.make_async_remote_copy(
                m_out.at[stage],
                slots.at[source],
                sems.at[0, k],
                sems.at[1, source],
                device_id={axis: source},
                device_id_type=MESH,
            ).wait_recv()
        total = slots[0]
        for i in range(1, count):
            total = total + slots[i]
        return total

    stages = (
        (0, "gx", gx, ngx, m_gx, m_gx_sem),
        (1, "gy", gy, ngy, m_gy, m_gy_sem),
        (2, "map", z, n, m_map, m_map_sem),
    )

    def gather_step(step, carry):
        for sub in range(SUBS):
            acw_copy(step - 1, sub).wait_recv()
            acw_copy(step, sub).start()
            accw_copy(step - 1, sub).wait_recv()
            accw_copy(step, sub).start()
        return carry

    mass_start(*stages[0], partial)
    third = max(1, (close - 1) // 3)
    points = [1, min(1 + third, close), min(1 + 2 * third, close), close]
    for i in range(3):
        lax.fori_loop(points[i], points[i + 1], gather_step, 0)
        total = mass_finish(*stages[i])
        if i < 2:
            mass_start(*stages[i + 1], total)
    for step in range(max(close, 1), far):
        for sub in range(SUBS):
            acw_copy(step - 1, sub).wait_recv()
            acw_copy(step, sub).start()
    for sub in range(SUBS):
        acw_copy(far - 1, sub).wait_recv()
        if close > 0:
            accw_copy(close - 1, sub).wait_recv()

    cells = float(rows * cols * ngx * ngy)
    norm_ref[...] = jnp.full((8, LANES), cells, jnp.float32) / jnp.sum(total)

    for dx, dy, ok in near:

        @pl.when(ok)
        def _():
            if dy == 0:
                for copy in row_copies(dx):
                    copy.wait_send()
            else:
                col_copy(dx, dy).wait_send()

    def drain_cw(step, carry):
        for sub in range(SUBS):
            cw_copy(cw.at[0, :, lanes(sub)], step, sub).wait_send()
            acw_copy(step, sub).wait_send()
        return carry

    def drain_ccw(step, carry):
        for sub in range(SUBS):
            ccw_copy(ccw.at[0, :, lanes(sub)], step, sub).wait_send()
            accw_copy(step, sub).wait_send()
        return carry

    lax.fori_loop(0, far, drain_cw, 0)
    lax.fori_loop(0, close, drain_ccw, 0)
    for stage in stages:
        for copy in mass_copies(*stage):
            copy.wait_send()


def step(sizes, densities, scaling, weights):
    n, ngx, ngy = sizes
    _, rows, cols = densities.shape
    wide = 2 * HALF
    frame = cols + 2 * LANES
    far, close = n // 2, max((n - 1) // 2, 1)
    size = rows // n
    brow1 = jnp.asarray(band(rows + wide, rows + 2 * wide, HALF))
    brow2 = jnp.asarray(band(rows, rows + wide, HALF))
    bcol = jnp.asarray(np.swapaxes(band(BLOCK, 2 * BLOCK, LANES), 1, 2))
    field = jax.ShapeDtypeStruct((rows, cols), jnp.float32)
    vmem = pl.BlockSpec(memory_space=pltpu.VMEM)
    hbm = pl.BlockSpec(memory_space=pl.ANY)
    dma = pltpu.SemaphoreType.DMA
    f32, bf16 = jnp.float32, jnp.bfloat16
    raw, ku, norm = pl.pallas_call(
        functools.partial(kernel, sizes, rows, cols),
        out_shape=(field, field, jax.ShapeDtypeStruct((8, LANES), f32)),
        in_specs=[hbm, hbm, pl.BlockSpec(memory_space=pltpu.SMEM), vmem, vmem, vmem],
        out_specs=(vmem, vmem, vmem),
        scratch_shapes=[
            pltpu.VMEM((rows + 2 * wide, frame), f32),
            pltpu.VMEM((rows + wide, frame), f32),
            pltpu.VMEM((rows + wide, frame), bf16),
            pltpu.VMEM((rows + wide, frame), bf16),
            pltpu.VMEM((rows + wide, frame), bf16),
            pltpu.VMEM((rows + wide, frame), bf16),
            pltpu.VMEM((rows, cols), f32),
            pltpu.VMEM((2, rows, LANES), f32),
            pltpu.VMEM((2, rows + 2 * wide, LANES), f32),
            pltpu.VMEM((far, size, cols), f32),
            pltpu.VMEM((close, size, cols), f32),
            pltpu.VMEM((3, 8, LANES), f32),
            pltpu.VMEM((ngx, 8, LANES), f32),
            pltpu.VMEM((ngy, 8, LANES), f32),
            pltpu.VMEM((n, 8, LANES), f32),
            dma((2,)),
            dma((10,)),
            dma((10,)),
            dma((far, SUBS)),
            dma((far, SUBS)),
            dma((close, SUBS)),
            dma((close, SUBS)),
            dma((far, SUBS)),
            dma((far, SUBS)),
            dma((close, SUBS)),
            dma((close, SUBS)),
            dma((2, ngx)),
            dma((2, ngy)),
            dma((2, n)),
        ],
        compiler_params=pltpu.CompilerParams(
            collective_id=0, has_side_effects=True, vmem_limit_bytes=48 * 1024 * 1024
        ),
        name="sinkhorn",
    )(scaling, densities, weights, brow1, brow2, bcol)
    barycenter = raw * norm[0, 0]
    new_scaling = barycenter / ku
    return barycenter, new_scaling[None]


def solution(mesh):
    placed = (P("map", "gx", "gy"), P("map", "gx", "gy"), P("map"))
    sizes = (mesh.shape["map"], mesh.shape["gx"], mesh.shape["gy"])
    return jax.shard_map(
        functools.partial(step, sizes),
        mesh=mesh,
        in_specs=placed,
        out_specs=(P("gx", "gy"), P("map", "gx", "gy")),
        check_vma=False,
    )
```

time: 331 us -> 106 us (0.32)
  waiting for transfers between devices: 156 us -> 0 us
  Pallas kernels: 0 us -> 97.6 us
  blocking collectives: 63.7 us -> 0 us
  starting transfers between devices: 32.1 us -> 0 us
  matrix products: 24.4 us -> 0 us
  local copies, waits for them, and re-layouts: 25.4 us -> 3.87 us
  between operations: 15 us -> 1.3 us
  other arithmetic: 13.2 us -> 2.67 us
    psum x1 -> x0, waiting for transfers between devices: 147 us -> none  [local(): logsum = lax.psum(partial_log, 'map')]
    pallas_call x0 -> x1, Pallas kernels: none -> 97.6 us  [step(): pl.pallas_call(functools.partial(kernel, sizes, rows, cols), out_shape=(f...]
    psum x1 -> x0, blocking collectives: 63.7 us -> none  [local(): mass = lax.psum(jnp.sum(raw), ('gx', 'gy'))]
    ppermute x8 -> x0, starting transfers between devices: 32.1 us -> none  [the longest x4 21.3 us: extended(): lax.ppermute(lax.slice_in_dim(block, 0, width, axis=dim), axis, backward)]
    dot_general x8 -> x0, matrix products: 24.4 us -> none  [the longest x4 12.8 us: smooth_axis(): jnp.einsum('ic,mbcj->mbij', small, piece, precision=lax.Precision.HIGHEST...]
    slice x12 -> x1, local copies, waits for them, and re-layouts: 11.6 us -> 0.52 us  [step(): barycenter = raw * norm[0, 0]]
    ppermute x8 -> x0, waiting for transfers between devices: 8.33 us -> none  [the longest x4 4.96 us: extended(): lax.ppermute(lax.slice_in_dim(block, 0, width, axis=dim), axis, backward)]
    reduce_sum x3 -> x0, other arithmetic: 5.92 us -> none  [the longest x1 2.88 us: local(): jnp.sum(weights[:, None, None] * jnp.log(scaling * ku), axis=0)]
  transfers between devices with their start and end apart: 9 -> 0, of which waited for: 9 -> 0; matrix products, arithmetic and copies ran while one was open for 1% -> 0% of each run, Pallas kernels for 0% -> 0%
where the time goes in v1:
time: 106 us; the launch traced here: 105 us
  Pallas kernels  97.6 us (92%)
  local copies, waits for them, and re-layouts  3.87 us (4%)
  other arithmetic  2.67 us (3%)
  between operations  1.3 us (1%)
    pallas_call x1, Pallas kernels, step(): pl.pallas_call(functools.partial(kernel, sizes, rows, cols), out_shape=(f...  97.6 us
    unnamed x6, local copies, waits for them, and re-layouts  3.35 us
    broadcast_in_dim x1, other arithmetic, step(): return (barycenter, new_scaling[None])  2.67 us

profile of v1, /device:TPU:6, one launch (start us, length us, event | category | flops | bytes accessed | tf_op | source)
XLA Modules:
  0.0 105.4 jit_solution(18144844300867994420)
XLA Ops:
  1.3 0.0 copy-start
  1.3 1.2 %copy-done = bf16[2,448,512]{2,1,0:T(8,128)(2,1)S(1)} copy-done((bf16[2,448,512]{2,1,0:T(8,128)(2,1)S(1)}, bf16[2,448,512]{2,1,0:T(8,128)(2,1)}, u32[]{:S(2)}) %copy-start) | copy-done | bytes 917528
  2.5 0.0 copy-start.1
  2.5 1.1 %copy-done.1 = bf16[2,384,448]{2,1,0:T(8,128)(2,1)S(1)} copy-done((bf16[2,384,448]{2,1,0:T(8,128)(2,1)S(1)}, bf16[2,384,448]{2,1,0:T(8,128)(2,1)}, u32[]{:S(2)}) %copy-start.1) | copy-done | bytes 688152
  3.6 0.0 copy-start.2
  3.6 1.0 copy-done.2
  4.6 97.6 %sinkhorn.1 = (f32[384,1024]{1,0:T(8,128)S(1)}, f32[384,1024]{1,0:T(8,128)S(1)}, f32[8,128]{1,0:T(8,128)S(1)}) custom-call(f32[1,384,1024]{2,1,0:T(8,128)} %s_hbm.1, f32[1,384,1024]{2,1,0:T(8,128)} %d_hbm.1, f32[1]{0:T(128)S(6)} %copy.8.w_ref, bf16[2,448,512]{2,1,0:T(8,128)(2,1)S(1)} %copy-done, bf16[2,384,448]{2,1,0:T(8,128)(2,1)S(1)} %copy-done.1, ...), custom_call_target="tpu_custom_call" | custom-call | tf_op jit(solution)/shard_map/sinkhorn/pallas_call | solution.py:511
  102.2 0.5 slice.3
  102.7 2.7 %divide_bitcast_fusion = (f32[1,384,1024]{2,1,0:T(8,128)}, f32[384,1024]{1,0:T(8,128)}) fusion(f32[384,1024]{1,0:T(8,128)S(1)} %get-tuple-element.7, f32[384,1024]{1,0:T(8,128)S(1)} %get-tuple-element.5, f32[]{:T(128)} %bitcast), kind=kLoop, calls=%fused_computation | loop fusion | flops 786432 | bytes 6291460 | tf_op jit(solution)/shard_map/broadcast_in_dim | solution.py:554
Async XLA Ops:
  1.3 1.2 %copy-start = (bf16[2,448,512]{2,1,0:T(8,128)(2,1)S(1)}, bf16[2,448,512]{2,1,0:T(8,128)(2,1)}, u32[]{:S(2)}) copy-start(bf16[2,448,512]{2,1,0:T(8,128)(2,1)} %constant.6.clone.brow1) | copy-start | bytes 2752516
  2.5 1.1 %copy-start.1 = (bf16[2,384,448]{2,1,0:T(8,128)(2,1)S(1)}, bf16[2,384,448]{2,1,0:T(8,128)(2,1)}, u32[]{:S(2)}) copy-start(bf16[2,384,448]{2,1,0:T(8,128)(2,1)} %constant.7.clone.brow2) | copy-start | bytes 2064388
  3.6 1.0 copy-start.2

commit v2 on v1

v2 whole, which is shorter than its diff:
```python
import functools

import jax
import jax.numpy as jnp
import numpy as np
from jax import lax
from jax.experimental import pallas as pl
from jax.experimental.pallas import tpu as pltpu
from jax.sharding import PartitionSpec as P

HALF = 32
SIGMA = 16
LANES = 128
BLOCK = 256
SUBS = 4
WINDOW = 4
MESH = pl.DeviceIdType.MESH


TAPS = np.arange(-HALF, HALF + 1, dtype=np.float64)
TOTAL = float(np.sum(np.exp(-TAPS * TAPS / (2.0 * SIGMA * SIGMA))))


def band(shape, shift):
    offset = (
        lax.broadcasted_iota(jnp.int32, shape, 1)
        - lax.broadcasted_iota(jnp.int32, shape, 0)
        + shift
    )
    distance = offset.astype(jnp.float32)
    values = jnp.exp(distance * distance * (-1.0 / (2.0 * SIGMA * SIGMA))) * (1.0 / TOTAL)
    return split(jnp.where(jnp.abs(offset) <= HALF, values, jnp.float32(0.0)))


def split(x):
    high = x.astype(jnp.bfloat16)
    low = (x - high.astype(jnp.float32)).astype(jnp.bfloat16)
    return high, low


def dot(a, b):
    return jnp.dot(a, b, preferred_element_type=jnp.float32)


def dot3(a_high, a_low, b_high, b_low):
    return dot(a_high, b_high) + (dot(a_high, b_low) + dot(a_low, b_high))


def kernel(
    sizes,
    rows,
    cols,
    s_hbm,
    d_hbm,
    w_ref,
    raw_ref,
    ku_ref,
    norm_ref,
    brow,
    bedge,
    bcol,
    field,
    dens,
    edge,
    pack,
    strip,
    corner,
    y_high,
    y_low,
    y_edge,
    term,
    long,
    short,
    m_out,
    m_gx,
    m_gy,
    m_map,
    in_sem,
    halo_send,
    halo_recv,
    long_send,
    long_recv,
    short_send,
    short_recv,
    along_send,
    along_recv,
    ashort_send,
    ashort_recv,
    m_gx_sem,
    m_gy_sem,
    m_map_sem,
):
    n, ngx, ngy = sizes
    z, gx, gy = lax.axis_index("map"), lax.axis_index("gx"), lax.axis_index("gy")
    main = pl.ds(0, cols)
    quarter = rows // 4
    low_rows, high_rows = pl.ds(0, HALF), pl.ds(rows - HALF, HALF)
    first_tile, last_tile = pl.ds(0, LANES), pl.ds(cols - LANES, LANES)
    halo_tile = pl.ds(cols, LANES)

    load_s = pltpu.make_async_copy(s_hbm.at[0], field.at[0, :, main], in_sem.at[0])
    load_d = pltpu.make_async_copy(d_hbm.at[0], dens, in_sem.at[1])
    load_s.start()
    load_d.start()

    near = []
    for dx in (-1, 0, 1):
        for dy in (-1, 0, 1):
            if dx or dy:
                ok = (gx + dx >= 0) & (gx + dx < ngx) & (gy + dy >= 0) & (gy + dy < ngy)
                near.append((dx, dy, ok))

    barrier = pltpu.get_barrier_semaphore()
    expected = jnp.int32(0)
    for dx, dy, ok in near:
        expected = expected + ok.astype(jnp.int32)

        @pl.when(ok)
        def _():
            pl.semaphore_signal(
                barrier, inc=1, device_id={"gx": gx + dx, "gy": gy + dy}, device_id_type=MESH
            )

    for axis, me, count in (("gx", gx, ngx), ("gy", gy, ngy), ("map", z, n)):
        for k in range(1, count):
            pl.semaphore_signal(
                barrier,
                inc=1,
                device_id={axis: lax.rem(me + k, count)},
                device_id_type=MESH,
            )
        expected = expected + (count - 1)

    def slot(delta):
        return 0 if delta < 0 else 1

    for dx, dy, ok in near:

        @pl.when(jnp.logical_not(ok))
        def _():
            for phase in range(2):
                if dy == 0:
                    edge[phase, slot(dx), :, main] = jnp.zeros((HALF, cols), jnp.float32)
                elif dx == 0:
                    strip[phase, slot(dy)] = jnp.zeros((quarter, LANES), jnp.float32)
                else:
                    corner[phase, slot(dx), slot(dy)] = jnp.zeros((HALF, LANES), jnp.float32)

    pl.semaphore_wait(barrier, expected)

    def halo_copy(phase, dx, dy):
        if dy == 0:
            source = s_hbm.at[0] if phase == 0 else field.at[1, :, main]
            source = source.at[low_rows if dx < 0 else high_rows]
            target = edge.at[phase, slot(-dx), :, main]
            index = slot(dx)
        elif dx == 0:
            source = pack.at[phase, slot(dy)]
            target = strip.at[phase, slot(-dy)]
            index = 2 + slot(dy)
        else:
            source = field.at[
                phase, low_rows if dx < 0 else high_rows, first_tile if dy < 0 else last_tile
            ]
            target = corner.at[phase, slot(-dx), slot(-dy)]
            index = 4 + 2 * slot(dx) + slot(dy)
        return pltpu.make_async_remote_copy(
            source,
            target,
            halo_send.at[phase, index],
            halo_recv.at[phase, index],
            device_id={"gx": gx + dx, "gy": gy + dy},
            device_id_type=MESH,
        )

    def halo_start(phase, which):
        for dx, dy, ok in near:
            if which(dx, dy):

                @pl.when(ok)
                def _():
                    halo_copy(phase, dx, dy).start()

    lane = lax.broadcasted_iota(jnp.int32, (quarter, LANES), 1)

    def rolled(value, shift):
        return pltpu.roll(value, shift % LANES, 1) if shift % LANES else value

    def pack_strips(phase):
        for q in range(4):
            at = pl.ds(q * quarter, quarter)
            here = (lane >= q * HALF) & (lane < (q + 1) * HALF)
            begin = rolled(field[phase, at, first_tile], q * HALF)
            end = rolled(field[phase, at, last_tile], (q + 1) * HALF)
            if q == 0:
                begin_all, end_all = begin, end
            else:
                begin_all = jnp.where(here, begin, begin_all)
                end_all = jnp.where(here, end, end_all)
        pack[phase, 0] = begin_all
        pack[phase, 1] = end_all

    def joined(left, right, lane):
        zero = jnp.float32(0.0)
        return jnp.where(lane >= LANES - HALF, left, jnp.where(lane < HALF, right, zero))

    def halo_finish(phase):
        for dx, dy, ok in near:
            @pl.when(ok)
            def _():
                halo_copy(phase, -dx, -dy).wait_recv()

        for q in range(4):
            left = rolled(strip[phase, 0], -(q + 1) * HALF)
            right = rolled(strip[phase, 1], -q * HALF)
            field[phase, pl.ds(q * quarter, quarter), halo_tile] = joined(left, right, lane)
        lane_corner = lax.broadcasted_iota(jnp.int32, (HALF, LANES), 1)
        for above in range(2):
            edge[phase, above, :, halo_tile] = joined(
                corner[phase, above, 0], corner[phase, above, 1], lane_corner
            )

    frame = cols + 2 * LANES

    def put(at_rows, at_cols, value):
        y_high[at_rows, at_cols], y_low[at_rows, at_cols] = split(value)

    def row_own(phase):
        def body(block, carry):
            base = pl.multiple_of(block * BLOCK, BLOCK)
            at = pl.ds(base, BLOCK)
            out = dot3(brow[0], brow[1], *split(field[phase, :, at]))
            put(pl.ds(0, rows), pl.ds(pl.multiple_of(base + LANES, LANES), BLOCK), out)
            y_edge[0, :, at] = out[:HALF]
            y_edge[1, :, at] = out[rows - HALF :]
            return carry

        lax.fori_loop(0, cols // BLOCK, body, 0)

    def row_halo(phase):
        out = dot3(brow[0], brow[1], *split(field[phase, :, halo_tile]))
        y_edge[0, :, halo_tile] = out[:HALF]
        y_edge[1, :, halo_tile] = out[rows - HALF :]
        for at in (0, cols + LANES):
            put(pl.ds(0, rows), pl.ds(at, LANES), out)
        for above, at_rows in ((0, low_rows), (1, high_rows)):
            more = dot3(bedge[above, 0], bedge[above, 1], *split(edge[phase, above]))
            total = y_edge[above] + more
            put(at_rows, pl.ds(LANES, cols + LANES), total)
            put(at_rows, pl.ds(0, LANES), total[:, cols:])

    def col_pass(base):
        source = pl.ds(base, 2 * BLOCK)
        return dot3(y_high[:, source], y_low[:, source], bcol[0], bcol[1])

    halo_start(0, lambda dx, dy: dy == 0)
    load_s.wait()
    pack_strips(0)
    halo_start(0, lambda dx, dy: dy != 0)
    brow[0], brow[1] = band((rows, rows), 0)
    for above, shift in ((0, -HALF), (1, HALF)):
        bedge[above, 0], bedge[above, 1] = band((HALF, HALF), shift)
    bcol[0], bcol[1] = band((2 * BLOCK, BLOCK), LANES)
    row_own(0)
    halo_finish(0)
    row_halo(0)
    load_d.wait()

    def u_block(block, carry):
        base = pl.multiple_of(block * BLOCK, BLOCK)
        at = pl.ds(base, BLOCK)
        field[1, :, at] = dens[:, at] / col_pass(base)
        return carry

    lax.fori_loop(0, cols // BLOCK, u_block, 0)
    halo_start(1, lambda dx, dy: dy == 0)
    pack_strips(1)
    halo_start(1, lambda dx, dy: dy != 0)
    row_own(1)
    halo_finish(1)
    row_halo(1)
    weight = w_ref[0]

    def ku_block(block, carry):
        base = pl.multiple_of(block * BLOCK, BLOCK)
        at = pl.ds(base, BLOCK)
        ku = col_pass(base)
        ku_ref[:, at] = ku
        term[:, at] = weight * jnp.log(field[0, :, at] * ku)
        return carry

    lax.fori_loop(0, cols // BLOCK, ku_block, 0)

    size = rows // n
    width = cols // SUBS
    far, close = n // 2, (n - 1) // 2
    after, before = lax.rem(z + 1, n), lax.rem(z + n - 1, n)

    def chunk(d):
        return pl.ds(pl.multiple_of(lax.rem(d + 2 * n, n) * size, 8), size)

    def lanes(sub):
        return pl.ds(sub * width, width)

    def target(sub, up):
        return {"map": after if (sub % 2 == 0) == up else before}

    def toward(sub, hops):
        return z + hops if sub % 2 == 0 else z - hops

    def long_copy(src, step, sub):
        return pltpu.make_async_remote_copy(
            src,
            long.at[step, :, lanes(sub)],
            long_send.at[step, sub],
            long_recv.at[step, sub],
            device_id=target(sub, True),
            device_id_type=MESH,
        )

    def short_copy(src, step, sub):
        return pltpu.make_async_remote_copy(
            src,
            short.at[step, :, lanes(sub)],
            short_send.at[step, sub],
            short_recv.at[step, sub],
            device_id=target(sub, False),
            device_id_type=MESH,
        )

    def long_next(step, sub):
        ref = long.at[step - 1, :, lanes(sub)]
        long_copy(ref, step - 1, sub).wait_recv()
        ref[...] += term[chunk(toward(sub, far - step)), lanes(sub)]
        return long_copy(ref, step, sub)

    def short_next(step, sub):
        ref = short.at[step - 1, :, lanes(sub)]
        short_copy(ref, step - 1, sub).wait_recv()
        ref[...] += term[chunk(toward(sub, step - close)), lanes(sub)]
        return short_copy(ref, step, sub)

    def send(step, sub, copy, same):
        back = sub - WINDOW
        if back >= 0:
            same(step, back).wait_send()
        else:
            @pl.when(step > 0)
            def _():
                same(step - 1, back + SUBS).wait_send()
        copy.start()

    def long_left(step, sub):
        return long_copy(long.at[0, :, lanes(sub)], step, sub)

    def short_left(step, sub):
        return short_copy(short.at[0, :, lanes(sub)], step, sub)

    for sub in range(SUBS):
        send(0, sub, long_copy(term.at[chunk(toward(sub, far)), lanes(sub)], 0, sub), long_left)
        send(0, sub, short_copy(term.at[chunk(toward(sub, -close)), lanes(sub)], 0, sub), short_left)

    def ring(step, carry):
        for sub in range(SUBS):
            send(step, sub, long_next(step, sub), long_left)
            send(step, sub, short_next(step, sub), short_left)
        return carry

    lax.fori_loop(1, close, ring, 0)
    for step in range(close, far):
        for sub in range(SUBS):
            send(step, sub, long_next(step, sub), long_left)

    def along_copy(step, sub):
        ref = raw_ref.at[chunk(toward(sub, -step)), lanes(sub)]
        return pltpu.make_async_remote_copy(
            ref,
            ref,
            along_send.at[step, sub],
            along_recv.at[step, sub],
            device_id=target(sub, True),
            device_id_type=MESH,
        )

    def ashort_copy(step, sub):
        ref = raw_ref.at[chunk(toward(sub, step)), lanes(sub)]
        return pltpu.make_async_remote_copy(
            ref,
            ref,
            ashort_send.at[step, sub],
            ashort_recv.at[step, sub],
            device_id=target(sub, False),
            device_id_type=MESH,
        )

    partial = jnp.zeros((8, LANES), jnp.float32)
    for sub in range(SUBS):
        long_left(far - 1, sub).wait_recv()
        short_left(close - 1, sub).wait_recv()
        value = term[chunk(z), lanes(sub)] + long[far - 1, :, lanes(sub)]
        value = jnp.exp(value + short[close - 1, :, lanes(sub)])
        raw_ref[chunk(z), lanes(sub)] = value
        send(0, sub, along_copy(0, sub), along_copy)
        send(0, sub, ashort_copy(0, sub), ashort_copy)
        for i in range(size // 8):
            for j in range(width // LANES):
                partial = partial + value[
                    i * 8 : (i + 1) * 8, j * LANES : (j + 1) * LANES
                ]

    def mass_copies(stage, axis, me, count, slots, sems):
        return [
            pltpu.make_async_remote_copy(
                m_out.at[stage],
                slots.at[me],
                sems.at[0, k],
                sems.at[1, me],
                device_id={axis: lax.rem(me + k, count)},
                device_id_type=MESH,
            )
            for k in range(1, count)
        ]

    def mass_start(stage, axis, me, count, slots, sems, value):
        m_out[stage] = value
        slots[me] = value
        for copy in mass_copies(stage, axis, me, count, slots, sems):
            copy.start()

    def mass_finish(stage, axis, me, count, slots, sems):
        for k in range(1, count):
            source = lax.rem(me + k, count)
            pltpu.make_async_remote_copy(
                m_out.at[stage],
                slots.at[source],
                sems.at[0, k],
                sems.at[1, source],
                device_id={axis: source},
                device_id_type=MESH,
            ).wait_recv()
        total = slots[0]
        for i in range(1, count):
            total = total + slots[i]
        return total

    stages = (
        (0, "gx", gx, ngx, m_gx, m_gx_sem),
        (1, "gy", gy, ngy, m_gy, m_gy_sem),
        (2, "map", z, n, m_map, m_map_sem),
    )

    def gather_step(step, carry):
        for sub in range(SUBS):
            along_copy(step - 1, sub).wait_recv()
            send(step, sub, along_copy(step, sub), along_copy)
            ashort_copy(step - 1, sub).wait_recv()
            send(step, sub, ashort_copy(step, sub), ashort_copy)
        return carry

    mass_start(*stages[0], partial)
    third = max(1, (close - 1) // 3)
    points = [1, min(1 + third, close), min(1 + 2 * third, close), close]
    for i in range(3):
        lax.fori_loop(points[i], points[i + 1], gather_step, 0)
        total = mass_finish(*stages[i])
        if i < 2:
            mass_start(*stages[i + 1], total)
    for step in range(close, far):
        for sub in range(SUBS):
            along_copy(step - 1, sub).wait_recv()
            send(step, sub, along_copy(step, sub), along_copy)
    for sub in range(SUBS):
        along_copy(far - 1, sub).wait_recv()
        ashort_copy(close - 1, sub).wait_recv()

    cells = float(rows * cols * ngx * ngy)
    norm_ref[...] = jnp.full((1, 1), cells, jnp.float32) / jnp.sum(total)

    for phase in range(2):
        for dx, dy, ok in near:

            @pl.when(ok)
            def _():
                halo_copy(phase, dx, dy).wait_send()

    for sub in range(SUBS - WINDOW, SUBS):
        long_left(far - 1, sub).wait_send()
        short_left(close - 1, sub).wait_send()
        along_copy(far - 1, sub).wait_send()
        ashort_copy(close - 1, sub).wait_send()
    for stage in stages:
        for copy in mass_copies(*stage):
            copy.wait_send()


def step(sizes, densities, scaling, weights):
    n, ngx, ngy = sizes
    _, rows, cols = densities.shape
    frame = cols + 2 * LANES
    far, close = n // 2, (n - 1) // 2
    size = rows // n
    out = jax.ShapeDtypeStruct((rows, cols), jnp.float32)
    vmem = pl.BlockSpec(memory_space=pltpu.VMEM)
    hbm = pl.BlockSpec(memory_space=pl.ANY)
    dma = pltpu.SemaphoreType.DMA
    f32, bf16 = jnp.float32, jnp.bfloat16
    raw, ku, norm = pl.pallas_call(
        functools.partial(kernel, sizes, rows, cols),
        out_shape=(out, out, jax.ShapeDtypeStruct((1, 1), f32)),
        in_specs=[hbm, hbm, pl.BlockSpec(memory_space=pltpu.SMEM)],
        out_specs=(vmem, vmem, vmem),
        scratch_shapes=[
            pltpu.VMEM((2, rows, rows), bf16),
            pltpu.VMEM((2, 2, HALF, HALF), bf16),
            pltpu.VMEM((2, 2 * BLOCK, BLOCK), bf16),
            pltpu.VMEM((2, rows, cols + LANES), f32),
            pltpu.VMEM((rows, cols), f32),
            pltpu.VMEM((2, 2, HALF, cols + LANES), f32),
            pltpu.VMEM((2, 2, rows // 4, LANES), f32),
            pltpu.VMEM((2, 2, rows // 4, LANES), f32),
            pltpu.VMEM((2, 2, 2, HALF, LANES), f32),
            pltpu.VMEM((rows, frame), bf16),
            pltpu.VMEM((rows, frame), bf16),
            pltpu.VMEM((2, HALF, cols + LANES), f32),
            pltpu.VMEM((rows, cols), f32),
            pltpu.VMEM((far, size, cols), f32),
            pltpu.VMEM((close, size, cols), f32),
            pltpu.VMEM((3, 8, LANES), f32),
            pltpu.VMEM((ngx, 8, LANES), f32),
            pltpu.VMEM((ngy, 8, LANES), f32),
            pltpu.VMEM((n, 8, LANES), f32),
            dma((2,)),
            dma((2, 8)),
            dma((2, 8)),
            dma((far, SUBS)),
            dma((far, SUBS)),
            dma((close, SUBS)),
            dma((close, SUBS)),
            dma((far, SUBS)),
            dma((far, SUBS)),
            dma((close, SUBS)),
            dma((close, SUBS)),
            dma((2, ngx)),
            dma((2, ngy)),
            dma((2, n)),
        ],
        compiler_params=pltpu.CompilerParams(
            collective_id=0, has_side_effects=True, vmem_limit_bytes=48 * 1024 * 1024
        ),
        name="sinkhorn",
    )(scaling, densities, weights)
    barycenter = raw * norm[0, 0]
    new_scaling = barycenter / ku
    return barycenter, new_scaling[None]


def solution(mesh):
    placed = (P("map", "gx", "gy"), P("map", "gx", "gy"), P("map"))
    sizes = (mesh.shape["map"], mesh.shape["gx"], mesh.shape["gy"])
    return jax.shard_map(
        functools.partial(step, sizes),
        mesh=mesh,
        in_specs=placed,
        out_specs=(P("gx", "gy"), P("map", "gx", "gy")),
        check_vma=False,
    )
```

time: 106 us -> 95.3 us (0.90)
  Pallas kernels: 97.6 us -> 89.8 us
  local copies, waits for them, and re-layouts: 3.87 us -> 1.4 us
    pallas_call x1, Pallas kernels: 97.6 us -> 89.8 us  [step(): pl.pallas_call(functools.partial(kernel, sizes, rows, cols), out_shape=(o...]
    unnamed x6 -> x2, local copies, waits for them, and re-layouts: 3.35 us -> 1.4 us
where the time goes in v2:
time: 95.3 us; the launch traced here: 95.2 us
  Pallas kernels  89.8 us (94%)
  other arithmetic  2.68 us (3%)
  local copies, waits for them, and re-layouts  1.4 us (1%)
  between operations  1.29 us (1%)
    pallas_call x1, Pallas kernels, step(): pl.pallas_call(functools.partial(kernel, sizes, rows, cols), out_shape=(o...  89.8 us
    broadcast_in_dim x1, other arithmetic, step(): return (barycenter, new_scaling[None])  2.68 us

profile of v2, /device:TPU:6, one launch (start us, length us, event | category | flops | bytes accessed | tf_op | source)
XLA Modules:
  0.0 95.2 jit_solution(15770324167665388654)
XLA Ops:
  1.3 0.0 copy-start
  1.3 1.4 %copy-done = f32[1,384,1024]{2,1,0:T(8,128)S(1)} copy-done((f32[1,384,1024]{2,1,0:T(8,128)S(1)}, f32[1,384,1024]{2,1,0:T(8,128)}, u32[]{:S(2)}) %copy-start) | copy-done | bytes 1572888
  2.7 89.8 %sinkhorn.1 = (f32[384,1024]{1,0:T(8,128)S(1)}, f32[384,1024]{1,0:T(8,128)S(1)}, f32[1,1]{1,0:T(1,128)}) custom-call(f32[1,384,1024]{2,1,0:T(8,128)S(1)} %copy-done, f32[1,384,1024]{2,1,0:T(8,128)} %d_hbm.1, f32[1]{0:T(128)S(6)} %copy.5.w_ref), custom_call_target="tpu_custom_call" | custom-call | tf_op jit(solution)/shard_map/sinkhorn/pallas_call | solution.py:507
  92.5 2.7 %divide_bitcast_fusion = (f32[1,384,1024]{2,1,0:T(8,128)}, f32[384,1024]{1,0:T(8,128)}) fusion(f32[384,1024]{1,0:T(8,128)S(1)} %get-tuple-element.7, f32[384,1024]{1,0:T(8,128)S(1)} %get-tuple-element.5, f32[]{:T(128)} %bitcast), kind=kLoop, calls=%fused_computation | loop fusion | flops 786432 | bytes 6291460 | tf_op jit(solution)/shard_map/broadcast_in_dim | solution.py:554
Async XLA Ops:
  1.3 1.4 %copy-start = (f32[1,384,1024]{2,1,0:T(8,128)S(1)}, f32[1,384,1024]{2,1,0:T(8,128)}, u32[]{:S(2)}) copy-start(f32[1,384,1024]{2,1,0:T(8,128)} %s_hbm.1) | copy-start | bytes 4718596

commit v3 on v2

--- a/solution.py
+++ b/solution.py
@@ -13,7 +13,7 @@
 LANES = 128
 BLOCK = 256
 SUBS = 4
-WINDOW = 4
+SKIPS = (2, 1)
 MESH = pl.DeviceIdType.MESH
 
 
@@ -69,8 +69,10 @@
     y_low,
     y_edge,
     term,
-    long,
-    short,
+    sums0,
+    sums1,
+    asides0,
+    asides1,
     m_out,
     m_gx,
     m_gy,
@@ -78,14 +80,14 @@
     in_sem,
     halo_send,
     halo_recv,
-    long_send,
-    long_recv,
-    short_send,
-    short_recv,
-    along_send,
-    along_recv,
-    ashort_send,
-    ashort_recv,
+    sum_sem0,
+    sum_sem1,
+    aside_sem0,
+    aside_sem1,
+    all_sem0,
+    all_sem1,
+    leaf_sem0,
+    leaf_sem1,
     m_gx_sem,
     m_gy_sem,
     m_map_sem,
@@ -289,12 +291,12 @@
         term[:, at] = weight * jnp.log(field[0, :, at] * ku)
         return carry
 
-    lax.fori_loop(0, cols // BLOCK, ku_block, 0)
-
     size = rows // n
     width = cols // SUBS
-    far, close = n // 2, (n - 1) // 2
-    after, before = lax.rem(z + 1, n), lax.rem(z + n - 1, n)
+    hops = (n // 2, (n - 1) // 2)
+    skips = SKIPS
+    plain = [hops[way] - 2 * skips[way] for way in range(2)]
+    steps = [hops[way] - skips[way] for way in range(2)]
 
     def chunk(d):
         return pl.ds(pl.multiple_of(lax.rem(d + 2 * n, n) * size, 8), size)
@@ -302,106 +304,100 @@
     def lanes(sub):
         return pl.ds(sub * width, width)
 
-    def target(sub, up):
-        return {"map": after if (sub % 2 == 0) == up else before}
-
-    def toward(sub, hops):
-        return z + hops if sub % 2 == 0 else z - hops
-
-    def long_copy(src, step, sub):
+    def toward(way, sub, distance):
+        return z + distance if (sub + way) % 2 == 0 else z - distance
+
+    def device(way, sub, distance):
+        return {"map": lax.rem(toward(way, sub, distance) + n, n)}
+
+    sums, asides = (sums0, sums1), (asides0, asides1)
+    sum_sems, aside_sems = (sum_sem0, sum_sem1), (aside_sem0, aside_sem1)
+    all_sems, leaf_sems = (all_sem0, all_sem1), (leaf_sem0, leaf_sem1)
+
+    def remote(source, target, sems, step, sub, to):
         return pltpu.make_async_remote_copy(
-            src,
-            long.at[step, :, lanes(sub)],
-            long_send.at[step, sub],
-            long_recv.at[step, sub],
-            device_id=target(sub, True),
+            source,
+            target,
+            sems.at[0, step, sub],
+            sems.at[1, step, sub],
+            device_id=to,
             device_id_type=MESH,
         )
 
-    def short_copy(src, step, sub):
-        return pltpu.make_async_remote_copy(
-            src,
-            short.at[step, :, lanes(sub)],
-            short_send.at[step, sub],
-            short_recv.at[step, sub],
-            device_id=target(sub, False),
-            device_id_type=MESH,
-        )
-
-    def long_next(step, sub):
-        ref = long.at[step - 1, :, lanes(sub)]
-        long_copy(ref, step - 1, sub).wait_recv()
-        ref[...] += term[chunk(toward(sub, far - step)), lanes(sub)]
-        return long_copy(ref, step, sub)
-
-    def short_next(step, sub):
-        ref = short.at[step - 1, :, lanes(sub)]
-        short_copy(ref, step - 1, sub).wait_recv()
-        ref[...] += term[chunk(toward(sub, step - close)), lanes(sub)]
-        return short_copy(ref, step, sub)
-
-    def send(step, sub, copy, same):
-        back = sub - WINDOW
-        if back >= 0:
-            same(step, back).wait_send()
-        else:
-            @pl.when(step > 0)
-            def _():
-                same(step - 1, back + SUBS).wait_send()
-        copy.start()
-
-    def long_left(step, sub):
-        return long_copy(long.at[0, :, lanes(sub)], step, sub)
-
-    def short_left(step, sub):
-        return short_copy(short.at[0, :, lanes(sub)], step, sub)
+    def role(way, step):
+        if step < plain[way]:
+            return hops[way] - step
+        return 2 * (skips[way] - (step - plain[way]))
+
+    def sum_copy(way, step, sub, source=None):
+        target = sums[way].at[step, :, lanes(sub)]
+        source = target if source is None else source
+        to = device(way, sub, 1 if step < plain[way] else 2)
+        return remote(source, target, sum_sems[way], step, sub, to)
+
+    def aside_copy(way, index, sub):
+        source = term.at[chunk(toward(way, sub, 2 * index + 1)), lanes(sub)]
+        target = asides[way].at[index, :, lanes(sub)]
+        return remote(source, target, aside_sems[way], index, sub, device(way, sub, 1))
+
+    def arrived(way, step, sub):
+        sum_copy(way, step - 1, sub).wait_recv()
+        value = sums[way][step - 1, :, lanes(sub)]
+        if step > plain[way]:
+            index = skips[way] - (step - plain[way])
+            aside_copy(way, index, sub).wait_recv()
+            value = value + asides[way][index, :, lanes(sub)]
+        return value
+
+    def sum_first(sub):
+        for way in range(2):
+            own = term.at[chunk(toward(way, sub, hops[way])), lanes(sub)]
+            sum_copy(way, 0, sub, own).start()
+
+    def sum_next(way, step, sub):
+        at = chunk(toward(way, sub, role(way, step)))
+        held = sums[way].at[step - 1, :, lanes(sub)]
+        held[...] = arrived(way, step, sub) + term[at, lanes(sub)]
+        sum_copy(way, step, sub, held).start()
+
+    for block in range(cols // BLOCK):
+        ku_block(block, 0)
+        for sub in range(SUBS):
+            if block * BLOCK < (sub + 1) * width <= (block + 1) * BLOCK:
+                sum_first(sub)
 
     for sub in range(SUBS):
-        send(0, sub, long_copy(term.at[chunk(toward(sub, far)), lanes(sub)], 0, sub), long_left)
-        send(0, sub, short_copy(term.at[chunk(toward(sub, -close)), lanes(sub)], 0, sub), short_left)
-
-    def ring(step, carry):
+        for way in range(2):
+            for index in range(skips[way]):
+                aside_copy(way, index, sub).start()
+    for step in range(1, max(steps)):
         for sub in range(SUBS):
-            send(step, sub, long_next(step, sub), long_left)
-            send(step, sub, short_next(step, sub), short_left)
-        return carry
-
-    lax.fori_loop(1, close, ring, 0)
-    for step in range(close, far):
-        for sub in range(SUBS):
-            send(step, sub, long_next(step, sub), long_left)
-
-    def along_copy(step, sub):
-        ref = raw_ref.at[chunk(toward(sub, -step)), lanes(sub)]
-        return pltpu.make_async_remote_copy(
-            ref,
-            ref,
-            along_send.at[step, sub],
-            along_recv.at[step, sub],
-            device_id=target(sub, True),
-            device_id_type=MESH,
-        )
-
-    def ashort_copy(step, sub):
-        ref = raw_ref.at[chunk(toward(sub, step)), lanes(sub)]
-        return pltpu.make_async_remote_copy(
-            ref,
-            ref,
-            ashort_send.at[step, sub],
-            ashort_recv.at[step, sub],
-            device_id=target(sub, False),
-            device_id_type=MESH,
-        )
+            for way in range(2):
+                if step < steps[way]:
+                    sum_next(way, step, sub)
+
+    def gather_copy(way, step, sub):
+        done = 2 * step if step <= skips[way] else step + skips[way]
+        ref = raw_ref.at[chunk(toward(way, sub, -done)), lanes(sub)]
+        to = device(way, sub, 2 if step < skips[way] else 1)
+        return remote(ref, ref, all_sems[way], step, sub, to)
+
+    def leaf_copy(way, index, sub):
+        ref = raw_ref.at[chunk(toward(way, sub, -2 * index)), lanes(sub)]
+        return remote(ref, ref, leaf_sems[way], index, sub, device(way, sub, 1))
+
+    def gather_start(way, step, sub):
+        gather_copy(way, step, sub).start()
+        if step < skips[way]:
+            leaf_copy(way, step, sub).start()
 
     partial = jnp.zeros((8, LANES), jnp.float32)
     for sub in range(SUBS):
-        long_left(far - 1, sub).wait_recv()
-        short_left(close - 1, sub).wait_recv()
-        value = term[chunk(z), lanes(sub)] + long[far - 1, :, lanes(sub)]
-        value = jnp.exp(value + short[close - 1, :, lanes(sub)])
+        value = term[chunk(z), lanes(sub)] + arrived(0, steps[0], sub)
+        value = jnp.exp(value + arrived(1, steps[1], sub))
         raw_ref[chunk(z), lanes(sub)] = value
-        send(0, sub, along_copy(0, sub), along_copy)
-        send(0, sub, ashort_copy(0, sub), ashort_copy)
+        for way in range(2):
+            gather_start(way, 0, sub)
         for i in range(size // 8):
             for j in range(width // LANES):
                 partial = partial + value[
@@ -449,29 +445,24 @@
         (2, "map", z, n, m_map, m_map_sem),
     )
 
-    def gather_step(step, carry):
+    mass_start(*stages[0], partial)
+    turns = [1 + (i + 1) * (max(steps) - 1) // 3 for i in range(3)]
+    for step in range(1, max(steps) + 1):
+        for i in range(3):
+            if step == turns[i]:
+                total = mass_finish(*stages[i])
+                if i < 2:
+                    mass_start(*stages[i + 1], total)
         for sub in range(SUBS):
-            along_copy(step - 1, sub).wait_recv()
-            send(step, sub, along_copy(step, sub), along_copy)
-            ashort_copy(step - 1, sub).wait_recv()
-            send(step, sub, ashort_copy(step, sub), ashort_copy)
-        return carry
-
-    mass_start(*stages[0], partial)
-    third = max(1, (close - 1) // 3)
-    points = [1, min(1 + third, close), min(1 + 2 * third, close), close]
-    for i in range(3):
-        lax.fori_loop(points[i], points[i + 1], gather_step, 0)
-        total = mass_finish(*stages[i])
-        if i < 2:
-            mass_start(*stages[i + 1], total)
-    for step in range(close, far):
-        for sub in range(SUBS):
-            along_copy(step - 1, sub).wait_recv()
-            send(step, sub, along_copy(step, sub), along_copy)
+            for way in range(2):
+                if step <= steps[way]:
+                    gather_copy(way, step - 1, sub).wait_recv()
+                if step < steps[way]:
+                    gather_start(way, step, sub)
     for sub in range(SUBS):
-        along_copy(far - 1, sub).wait_recv()
-        ashort_copy(close - 1, sub).wait_recv()
+        for way in range(2):
+            for index in range(skips[way]):
+                leaf_copy(way, index, sub).wait_recv()
 
     cells = float(rows * cols * ngx * ngy)
     norm_ref[...] = jnp.full((1, 1), cells, jnp.float32) / jnp.sum(total)
@@ -483,11 +474,14 @@
             def _():
                 halo_copy(phase, dx, dy).wait_send()
 
-    for sub in range(SUBS - WINDOW, SUBS):
-        long_left(far - 1, sub).wait_send()
-        short_left(close - 1, sub).wait_send()
-        along_copy(far - 1, sub).wait_send()
-        ashort_copy(close - 1, sub).wait_send()
+    for sub in range(SUBS):
+        for way in range(2):
+            for step in range(steps[way]):
+                sum_copy(way, step, sub).wait_send()
+                gather_copy(way, step, sub).wait_send()
+            for index in range(skips[way]):
+                aside_copy(way, index, sub).wait_send()
+                leaf_copy(way, index, sub).wait_send()
     for stage in stages:
         for copy in mass_copies(*stage):
             copy.wait_send()
@@ -497,8 +491,9 @@
     n, ngx, ngy = sizes
     _, rows, cols = densities.shape
     frame = cols + 2 * LANES
-    far, close = n // 2, (n - 1) // 2
     size = rows // n
+    steps = (n // 2 - SKIPS[0], (n - 1) // 2 - SKIPS[1])
+    extra = [max(k, 1) for k in SKIPS]
     out = jax.ShapeDtypeStruct((rows, cols), jnp.float32)
     vmem = pl.BlockSpec(memory_space=pltpu.VMEM)
     hbm = pl.BlockSpec(memory_space=pl.ANY)
@@ -523,8 +518,7 @@
             pltpu.VMEM((rows, frame), bf16),
             pltpu.VMEM((2, HALF, cols + LANES), f32),
             pltpu.VMEM((rows, cols), f32),
-            pltpu.VMEM((far, size, cols), f32),
-            pltpu.VMEM((close, size, cols), f32),
+            *[pltpu.VMEM((k, size, cols), f32) for k in (*steps, *extra)],
             pltpu.VMEM((3, 8, LANES), f32),
             pltpu.VMEM((ngx, 8, LANES), f32),
             pltpu.VMEM((ngy, 8, LANES), f32),
@@ -532,14 +526,8 @@
             dma((2,)),
             dma((2, 8)),
             dma((2, 8)),
-            dma((far, SUBS)),
-            dma((far, SUBS)),
-            dma((close, SUBS)),
-            dma((close, SUBS)),
-            dma((far, SUBS)),
-            dma((far, SUBS)),
-            dma((close, SUBS)),
-            dma((close, SUBS)),
+            *[dma((2, k, SUBS)) for k in (*steps, *extra)],
+            *[dma((2, k, SUBS)) for k in (*steps, *extra)],
             dma((2, ngx)),
             dma((2, ngy)),
             dma((2, n)),

time: 95.3 us -> 90.3 us (0.948)
  Pallas kernels: 89.8 us -> 84.4 us
    pallas_call x1, Pallas kernels: 89.8 us -> 84.4 us  [step(): pl.pallas_call(functools.partial(kernel, sizes, rows, cols), out_shape=(o...]
where the time goes in v3:
time: 90.3 us; the launch traced here: 89.8 us
  Pallas kernels  84.4 us (93%)
  other arithmetic  2.68 us (3%)
  local copies, waits for them, and re-layouts  1.4 us (2%)
  between operations  1.29 us (1%)
    pallas_call x1, Pallas kernels, step(): pl.pallas_call(functools.partial(kernel, sizes, rows, cols), out_shape=(o...  84.4 us
    broadcast_in_dim x1, other arithmetic, step(): return (barycenter, new_scaling[None])  2.68 us

profile of v3, /device:TPU:6, one launch (start us, length us, event | category | flops | bytes accessed | tf_op | source)
XLA Modules:
  0.0 89.8 jit_solution(9525775150144014415)
XLA Ops:
  1.3 0.0 copy-start
  1.3 1.4 %copy-done = f32[1,384,1024]{2,1,0:T(8,128)S(1)} copy-done((f32[1,384,1024]{2,1,0:T(8,128)S(1)}, f32[1,384,1024]{2,1,0:T(8,128)}, u32[]{:S(2)}) %copy-start) | copy-done | bytes 1572888
  2.7 84.4 %sinkhorn.1 = (f32[384,1024]{1,0:T(8,128)S(1)}, f32[384,1024]{1,0:T(8,128)S(1)}, f32[1,1]{1,0:T(1,128)}) custom-call(f32[1,384,1024]{2,1,0:T(8,128)S(1)} %copy-done, f32[1,384,1024]{2,1,0:T(8,128)} %d_hbm.1, f32[1]{0:T(128)S(6)} %copy.5.w_ref), custom_call_target="tpu_custom_call" | custom-call | tf_op jit(solution)/shard_map/sinkhorn/pallas_call | solution.py:502
  87.1 2.7 %divide_bitcast_fusion = (f32[1,384,1024]{2,1,0:T(8,128)}, f32[384,1024]{1,0:T(8,128)}) fusion(f32[384,1024]{1,0:T(8,128)S(1)} %get-tuple-element.7, f32[384,1024]{1,0:T(8,128)S(1)} %get-tuple-element.5, f32[]{:T(128)} %bitcast), kind=kLoop, calls=%fused_computation | loop fusion | flops 786432 | bytes 6291460 | tf_op jit(solution)/shard_map/broadcast_in_dim | solution.py:542
Async XLA Ops:
  1.3 1.4 %copy-start = (f32[1,384,1024]{2,1,0:T(8,128)S(1)}, f32[1,384,1024]{2,1,0:T(8,128)}, u32[]{:S(2)}) copy-start(f32[1,384,1024]{2,1,0:T(8,128)} %s_hbm.1) | copy-start | bytes 4718596

commit v4 on v3

--- a/solution.py
+++ b/solution.py
@@ -136,18 +136,6 @@
     def slot(delta):
         return 0 if delta < 0 else 1
 
-    for dx, dy, ok in near:
-
-        @pl.when(jnp.logical_not(ok))
-        def _():
-            for phase in range(2):
-                if dy == 0:
-                    edge[phase, slot(dx), :, main] = jnp.zeros((HALF, cols), jnp.float32)
-                elif dx == 0:
-                    strip[phase, slot(dy)] = jnp.zeros((quarter, LANES), jnp.float32)
-                else:
-                    corner[phase, slot(dx), slot(dy)] = jnp.zeros((HALF, LANES), jnp.float32)
-
     pl.semaphore_wait(barrier, expected)
 
     def halo_copy(phase, dx, dy):
@@ -259,6 +247,18 @@
     load_s.wait()
     pack_strips(0)
     halo_start(0, lambda dx, dy: dy != 0)
+    for dx, dy, ok in near:
+
+        @pl.when(jnp.logical_not(ok))
+        def _():
+            for phase in range(2):
+                if dy == 0:
+                    edge[phase, slot(dx), :, main] = jnp.zeros((HALF, cols), jnp.float32)
+                elif dx == 0:
+                    strip[phase, slot(dy)] = jnp.zeros((quarter, LANES), jnp.float32)
+                else:
+                    corner[phase, slot(dx), slot(dy)] = jnp.zeros((HALF, LANES), jnp.float32)
+
     brow[0], brow[1] = band((rows, rows), 0)
     for above, shift in ((0, -HALF), (1, HALF)):
         bedge[above, 0], bedge[above, 1] = band((HALF, HALF), shift)
@@ -366,15 +366,21 @@
             if block * BLOCK < (sub + 1) * width <= (block + 1) * BLOCK:
                 sum_first(sub)
 
-    for sub in range(SUBS):
+    def asides_after(step, sub):
         for way in range(2):
             for index in range(skips[way]):
-                aside_copy(way, index, sub).start()
+                use = steps[way] - index
+                if step == max(use - 4 + way, 0):
+                    aside_copy(way, index, sub).start()
+
+    for sub in range(SUBS):
+        asides_after(0, sub)
     for step in range(1, max(steps)):
         for sub in range(SUBS):
             for way in range(2):
                 if step < steps[way]:
                     sum_next(way, step, sub)
+            asides_after(step, sub)
 
     def gather_copy(way, step, sub):
         done = 2 * step if step <= skips[way] else step + skips[way]
@@ -388,8 +394,12 @@
 
     def gather_start(way, step, sub):
         gather_copy(way, step, sub).start()
-        if step < skips[way]:
-            leaf_copy(way, step, sub).start()
+
+    def leaves_after(step, sub):
+        for way in range(2):
+            for index in range(skips[way]):
+                if step == min(2 + index + 2 * way, max(steps) - 2):
+                    leaf_copy(way, index, sub).start()
 
     partial = jnp.zeros((8, LANES), jnp.float32)
     for sub in range(SUBS):
@@ -445,46 +455,63 @@
         (2, "map", z, n, m_map, m_map_sem),
     )
 
+    def halos_left():
+        for phase in range(2):
+            for dx, dy, ok in near:
+
+                @pl.when(ok)
+                def _():
+                    halo_copy(phase, dx, dy).wait_send()
+
+    def asides_left():
+        for sub in range(SUBS):
+            for way in range(2):
+                for index in range(skips[way]):
+                    aside_copy(way, index, sub).wait_send()
+
     mass_start(*stages[0], partial)
-    turns = [1 + (i + 1) * (max(steps) - 1) // 3 for i in range(3)]
+    turns = [1 + (i + 1) * (max(steps) - 1) // 3 for i in range(2)]
     for step in range(1, max(steps) + 1):
-        for i in range(3):
+        for i in range(2):
             if step == turns[i]:
                 total = mass_finish(*stages[i])
-                if i < 2:
-                    mass_start(*stages[i + 1], total)
+                mass_start(*stages[i + 1], total)
+                for copy in mass_copies(*stages[i]):
+                    copy.wait_send()
         for sub in range(SUBS):
             for way in range(2):
                 if step <= steps[way]:
                     gather_copy(way, step - 1, sub).wait_recv()
                 if step < steps[way]:
                     gather_start(way, step, sub)
+            leaves_after(step, sub)
+        if step == 1:
+            halos_left()
+        if step == 2:
+            asides_left()
+        for sub in range(SUBS):
+            for way in range(2):
+                if step - 1 < steps[way]:
+                    sum_copy(way, step - 1, sub).wait_send()
+                if 2 <= step < steps[way] + 2:
+                    gather_copy(way, step - 2, sub).wait_send()
     for sub in range(SUBS):
         for way in range(2):
             for index in range(skips[way]):
                 leaf_copy(way, index, sub).wait_recv()
 
+    total = mass_finish(*stages[2])
     cells = float(rows * cols * ngx * ngy)
     norm_ref[...] = jnp.full((1, 1), cells, jnp.float32) / jnp.sum(total)
 
-    for phase in range(2):
-        for dx, dy, ok in near:
-
-            @pl.when(ok)
-            def _():
-                halo_copy(phase, dx, dy).wait_send()
-
     for sub in range(SUBS):
         for way in range(2):
-            for step in range(steps[way]):
-                sum_copy(way, step, sub).wait_send()
-                gather_copy(way, step, sub).wait_send()
+            if max(steps) - 1 < steps[way]:
+                gather_copy(way, max(steps) - 1, sub).wait_send()
             for index in range(skips[way]):
-                aside_copy(way, index, sub).wait_send()
                 leaf_copy(way, index, sub).wait_send()
-    for stage in stages:
-        for copy in mass_copies(*stage):
-            copy.wait_send()
+    for copy in mass_copies(*stages[2]):
+        copy.wait_send()
 
 
 def step(sizes, densities, scaling, weights):
@@ -533,7 +560,7 @@
             dma((2, n)),
         ],
         compiler_params=pltpu.CompilerParams(
-            collective_id=0, has_side_effects=True, vmem_limit_bytes=48 * 1024 * 1024
+            collective_id=0, has_side_effects=True, vmem_limit_bytes=50 * 1024 * 1024
         ),
         name="sinkhorn",
     )(scaling, densities, weights)

time: 90.3 us -> 88.4 us (0.979)
  local copies, waits for them, and re-layouts: 1.4 us -> 0 us
    unnamed x2 -> x0, local copies, waits for them, and re-layouts: 1.4 us -> none
where the time goes in v4:
time: 88.4 us; the launch traced here: 88 us
  Pallas kernels  84 us (95%)
  other arithmetic  2.68 us (3%)
  between operations  1.28 us (1%)
    pallas_call x1, Pallas kernels, step(): pl.pallas_call(functools.partial(kernel, sizes, rows, cols), out_shape=(o...  84 us
    broadcast_in_dim x1, other arithmetic, step(): return (barycenter, new_scaling[None])  2.68 us

profile of v4, /device:TPU:6, one launch (start us, length us, event | category | flops | bytes accessed | tf_op | source)
XLA Modules:
  0.0 88.0 jit_solution(1135825299278491433)
XLA Ops:
  1.3 84.0 %sinkhorn.1 = (f32[384,1024]{1,0:T(8,128)S(1)}, f32[384,1024]{1,0:T(8,128)S(1)}, f32[1,1]{1,0:T(1,128)}) custom-call(f32[1,384,1024]{2,1,0:T(8,128)} %s_hbm.1, f32[1,384,1024]{2,1,0:T(8,128)} %d_hbm.1, f32[1]{0:T(128)S(6)} %copy.5.w_ref), custom_call_target="tpu_custom_call" | custom-call | tf_op jit(solution)/shard_map/sinkhorn/pallas_call | solution.py:529
  85.3 2.7 %divide_bitcast_fusion = (f32[1,384,1024]{2,1,0:T(8,128)}, f32[384,1024]{1,0:T(8,128)}) fusion(f32[384,1024]{1,0:T(8,128)S(1)} %get-tuple-element.7, f32[384,1024]{1,0:T(8,128)S(1)} %get-tuple-element.5, f32[]{:T(128)} %bitcast), kind=kLoop, calls=%fused_computation | loop fusion | flops 786432 | bytes 6291460 | tf_op jit(solution)/shard_map/broadcast_in_dim | solution.py:569

commit v5 on v4

--- a/solution.py
+++ b/solution.py
@@ -138,22 +138,23 @@
 
     pl.semaphore_wait(barrier, expected)
 
-    def halo_copy(phase, dx, dy):
+    def halo_copy(phase, dx, dy, block=0):
         if dy == 0:
-            source = s_hbm.at[0] if phase == 0 else field.at[1, :, main]
-            source = source.at[low_rows if dx < 0 else high_rows]
-            target = edge.at[phase, slot(-dx), :, main]
-            index = slot(dx)
+            at_rows = low_rows if dx < 0 else high_rows
+            at = pl.ds(block * BLOCK, BLOCK)
+            source = s_hbm.at[0, at_rows, at] if phase == 0 else field.at[1, at_rows, at]
+            target = edge.at[phase, slot(-dx), :, at]
+            index = 6 + 2 * block + slot(dx)
         elif dx == 0:
             source = pack.at[phase, slot(dy)]
             target = strip.at[phase, slot(-dy)]
-            index = 2 + slot(dy)
+            index = slot(dy)
         else:
             source = field.at[
                 phase, low_rows if dx < 0 else high_rows, first_tile if dy < 0 else last_tile
             ]
             target = corner.at[phase, slot(-dx), slot(-dy)]
-            index = 4 + 2 * slot(dx) + slot(dy)
+            index = 2 + 2 * slot(dx) + slot(dy)
         return pltpu.make_async_remote_copy(
             source,
             target,
@@ -163,9 +164,20 @@
             device_id_type=MESH,
         )
 
-    def halo_start(phase, which):
+    def pieces(dy):
+        return range(cols // BLOCK) if dy == 0 else range(1)
+
+    def rows_start(phase, block):
         for dx, dy, ok in near:
-            if which(dx, dy):
+            if dy == 0:
+
+                @pl.when(ok)
+                def _():
+                    halo_copy(phase, dx, dy, block).start()
+
+    def sides_start(phase):
+        for dx, dy, ok in near:
+            if dy != 0:
 
                 @pl.when(ok)
                 def _():
@@ -198,7 +210,8 @@
         for dx, dy, ok in near:
             @pl.when(ok)
             def _():
-                halo_copy(phase, -dx, -dy).wait_recv()
+                for block in pieces(dy):
+                    halo_copy(phase, -dx, -dy, block).wait_recv()
 
         for q in range(4):
             left = rolled(strip[phase, 0], -(q + 1) * HALF)
@@ -243,10 +256,11 @@
         source = pl.ds(base, 2 * BLOCK)
         return dot3(y_high[:, source], y_low[:, source], bcol[0], bcol[1])
 
-    halo_start(0, lambda dx, dy: dy == 0)
+    for block in pieces(0):
+        rows_start(0, block)
     load_s.wait()
     pack_strips(0)
-    halo_start(0, lambda dx, dy: dy != 0)
+    sides_start(0)
     for dx, dy, ok in near:
 
         @pl.when(jnp.logical_not(ok))
@@ -274,10 +288,15 @@
         field[1, :, at] = dens[:, at] / col_pass(base)
         return carry
 
-    lax.fori_loop(0, cols // BLOCK, u_block, 0)
-    halo_start(1, lambda dx, dy: dy == 0)
+    outer = list(dict.fromkeys((0, cols // BLOCK - 1)))
+    for block in outer:
+        u_block(block, 0)
+        rows_start(1, block)
     pack_strips(1)
-    halo_start(1, lambda dx, dy: dy != 0)
+    sides_start(1)
+    for block in range(1, cols // BLOCK - 1):
+        u_block(block, 0)
+        rows_start(1, block)
     row_own(1)
     halo_finish(1)
     row_halo(1)
@@ -461,7 +480,8 @@
 
                 @pl.when(ok)
                 def _():
-                    halo_copy(phase, dx, dy).wait_send()
+                    for block in pieces(dy):
+                        halo_copy(phase, dx, dy, block).wait_send()
 
     def asides_left():
         for sub in range(SUBS):
@@ -551,8 +571,8 @@
             pltpu.VMEM((ngy, 8, LANES), f32),
             pltpu.VMEM((n, 8, LANES), f32),
             dma((2,)),
-            dma((2, 8)),
-            dma((2, 8)),
+            dma((2, 6 + 2 * (cols // BLOCK))),
+            dma((2, 6 + 2 * (cols // BLOCK))),
             *[dma((2, k, SUBS)) for k in (*steps, *extra)],
             *[dma((2, k, SUBS)) for k in (*steps, *extra)],
             dma((2, ngx)),

time: 88.4 us -> 87 us (0.984)
  Pallas kernels: 84 us -> 82.3 us
    pallas_call x1, Pallas kernels: 84 us -> 82.3 us  [step(): pl.pallas_call(functools.partial(kernel, sizes, rows, cols), out_shape=(o...]
where the time goes in v5:
time: 87 us; the launch traced here: 86.3 us
  Pallas kernels  82.3 us (95%)
  other arithmetic  2.68 us (3%)
  between operations  1.28 us (1%)
    pallas_call x1, Pallas kernels, step(): pl.pallas_call(functools.partial(kernel, sizes, rows, cols), out_shape=(o...  82.3 us
    broadcast_in_dim x1, other arithmetic, step(): return (barycenter, new_scaling[None])  2.68 us

profile of v5, /device:TPU:6, one launch (start us, length us, event | category | flops | bytes accessed | tf_op | source)
XLA Modules:
  0.0 86.3 jit_solution(16311071107969716776)
XLA Ops:
  1.3 82.3 %sinkhorn.1 = (f32[384,1024]{1,0:T(8,128)S(1)}, f32[384,1024]{1,0:T(8,128)S(1)}, f32[1,1]{1,0:T(1,128)}) custom-call(f32[1,384,1024]{2,1,0:T(8,128)} %s_hbm.1, f32[1,384,1024]{2,1,0:T(8,128)} %d_hbm.1, f32[1]{0:T(128)S(6)} %copy.5.w_ref), custom_call_target="tpu_custom_call" | custom-call | tf_op jit(solution)/shard_map/sinkhorn/pallas_call | solution.py:549
  83.6 2.7 %divide_bitcast_fusion = (f32[1,384,1024]{2,1,0:T(8,128)}, f32[384,1024]{1,0:T(8,128)}) fusion(f32[384,1024]{1,0:T(8,128)S(1)} %get-tuple-element.7, f32[384,1024]{1,0:T(8,128)S(1)} %get-tuple-element.5, f32[]{:T(128)} %bitcast), kind=kLoop, calls=%fused_computation | loop fusion | flops 786432 | bytes 6291460 | tf_op jit(solution)/shard_map/broadcast_in_dim | solution.py:589

commit v6 on v5

--- a/solution.py
+++ b/solution.py
@@ -490,7 +490,7 @@
                     aside_copy(way, index, sub).wait_send()
 
     mass_start(*stages[0], partial)
-    turns = [1 + (i + 1) * (max(steps) - 1) // 3 for i in range(2)]
+    turns = [max(max(steps) - 3 + 2 * i, 1) for i in range(2)]
     for step in range(1, max(steps) + 1):
         for i in range(2):
             if step == turns[i]:

time: 87 us -> 87 us (level)
  no operation moved by 1% of the time
where the time goes in v6:
time: 87 us; the launch traced here: 86.3 us
  Pallas kernels  82.3 us (95%)
  other arithmetic  2.68 us (3%)
  between operations  1.28 us (1%)
    pallas_call x1, Pallas kernels, step(): pl.pallas_call(functools.partial(kernel, sizes, rows, cols), out_shape=(o...  82.3 us
    broadcast_in_dim x1, other arithmetic, step(): return (barycenter, new_scaling[None])  2.68 us

profile of v6, /device:TPU:6, one launch (start us, length us, event | category | flops | bytes accessed | tf_op | source)
XLA Modules:
  0.0 86.3 jit_solution(542184889635263937)
XLA Ops:
  1.3 82.3 %sinkhorn.1 = (f32[384,1024]{1,0:T(8,128)S(1)}, f32[384,1024]{1,0:T(8,128)S(1)}, f32[1,1]{1,0:T(1,128)}) custom-call(f32[1,384,1024]{2,1,0:T(8,128)} %s_hbm.1, f32[1,384,1024]{2,1,0:T(8,128)} %d_hbm.1, f32[1]{0:T(128)S(6)} %copy.5.w_ref), custom_call_target="tpu_custom_call" | custom-call | tf_op jit(solution)/shard_map/sinkhorn/pallas_call | solution.py:549
  83.6 2.7 %divide_bitcast_fusion = (f32[1,384,1024]{2,1,0:T(8,128)}, f32[384,1024]{1,0:T(8,128)}) fusion(f32[384,1024]{1,0:T(8,128)S(1)} %get-tuple-element.7, f32[384,1024]{1,0:T(8,128)S(1)} %get-tuple-element.5, f32[]{:T(128)} %bitcast), kind=kLoop, calls=%fused_computation | loop fusion | flops 786432 | bytes 6291460 | tf_op jit(solution)/shard_map/broadcast_in_dim | solution.py:589
